TPU v7x, 128 devices: a whole 4x4x4 slice. The times are simulated.
128 devices in a mesh: layer: 16 (over y, z_hi, core), feat: 8 (over x, z_lo).
Axes of the slice: x: 4, y: 4, z: 4 (z_hi: 2, z_lo: 2; z = z_hi * 2 + z_lo), core: 2. Of those that a mesh axis runs over, the one named last changes fastest.
Arguments:
- tokens_in: bfloat16 [512, 4096], P('feat', 'layer'), may hold values from -6 to 6
- targets: bfloat16 [512, 4096], P('feat', 'layer'), may hold values from -6 to 6
- enc_weight: bfloat16 [2048, 131072], P(None, ('layer', 'feat')), may hold values from -0.125 to 0.125
- enc_bias: float32 [131072], P(('layer', 'feat')), may hold values from -1 to 0.5
- dec_weight: bfloat16 [2, 131072, 2048], P(None, ('layer', 'feat')), may hold values from -0.0234375 to 0.0234375
Outputs:
- recon_error: float32 [512, 4096], P('feat', 'layer')
- mean_square: float32 [], replicated
- enc_grad: bfloat16 [2048, 131072], P(None, ('layer', 'feat'))
- bias_grad: float32 [131072], P(('layer', 'feat'))
- dec_grad: bfloat16 [2, 131072, 2048], P(None, ('layer', 'feat'))
All inputs are finite; a program needn't handle non-finite values.
Results may differ from a plain program's by a relative error of at most 0.02.
Values may be sent and summed in bfloat16 or wider, within the bound.
A program may use at most 128 MiB of HBM per device.

v0:
```python
import jax
import jax.numpy as jnp
from jax import lax
from jax.sharding import PartitionSpec as P

D = 2048
LAYERS = 2
TOK = 512


loss_scale = 64.0


def swapped(value, axis, stride):
    mask = 2**stride
    pairs = [(source, source ^ mask) for source in range(lax.axis_size(axis))]
    return lax.ppermute(value, axis, pairs)


def arrange_group(gathered, which_group, feat_count, sub_count):
    row_count = gathered.shape[1]
    col_count = gathered.shape[2]
    blocks = gathered.reshape(gathered.shape[0] // feat_count, feat_count, row_count, col_count)
    chosen = lax.dynamic_slice_in_dim(blocks, which_group * sub_count, sub_count, 0)
    return jnp.transpose(chosen, (1, 2, 0, 3)).reshape(
        feat_count * row_count, sub_count * col_count
    )


def order_pair(current, partner, member, bit_level, axis_dim):
    lower_first = member >> bit_level & 1 == 0
    leading = jnp.where(lower_first, current, partner)
    trailing = jnp.where(lower_first, partner, current)
    return jnp.concatenate([leading, trailing], axis_dim)


def on_device(tokens_in, targets, enc_weight, enc_bias, dec_weight):
    sub_count = lax.axis_size("layer") // LAYERS
    position = lax.axis_index("layer")
    layer_group = position // sub_count
    member = position % sub_count
    feat_count = lax.axis_size("feat")
    row_count = tokens_in.shape[0]
    col_count = tokens_in.shape[1]
    bit_count = sub_count.bit_length() - 1
    joined = tokens_in
    for bit_level in range(bit_count):
        partner = swapped(joined, "layer", bit_level)
        joined = order_pair(joined, partner, member, bit_level, 1)
    inputs = lax.all_gather(joined, "feat", axis=0, tiled=True)
    pre_act = jnp.dot(inputs, enc_weight, preferred_element_type=jnp.float32) + enc_bias
    features = jnp.maximum(pre_act, 0.0).astype(jnp.bfloat16)
    partial_value = jnp.einsum(
        "tf,kfd->tkd", features, dec_weight, preferred_element_type=jnp.float32
    )
    summed = lax.psum(partial_value.astype(jnp.bfloat16), "feat").astype(jnp.float32)
    summed_rows = lax.dynamic_slice_in_dim(summed, lax.axis_index("feat") * row_count, row_count, 0)
    gathered = lax.all_gather(
        summed_rows[None].astype(jnp.bfloat16), "layer", axis=0, tiled=True
    ).astype(jnp.float32)
    columns = lax.dynamic_slice_in_dim(gathered, member * col_count, col_count, 3)
    own_part = jnp.sum(
        lax.dynamic_slice_in_dim(columns, layer_group * sub_count, sub_count, 0)[:, :, 0, :], 0
    )
    prev_part = jnp.sum(
        lax.dynamic_slice_in_dim(
            columns, jnp.maximum(layer_group - 1, 0) * sub_count, sub_count, 0
        )[:, :, 1, :],
        0,
    )
    rebuilt = own_part + jnp.where(layer_group > 0, prev_part, 0.0)
    recon_error = rebuilt - targets.astype(jnp.float32)
    squares = lax.psum(jnp.sum(recon_error * recon_error), ("layer", "feat"))
    mean_square = squares / (LAYERS * TOK * D)
    scaled = (loss_scale / TOK * recon_error).astype(jnp.bfloat16)
    gathered = lax.all_gather(scaled[None], ("layer", "feat"), axis=0, tiled=True)
    own_grad = arrange_group(gathered, layer_group, feat_count, sub_count)
    next_index = jnp.minimum(layer_group + 1, LAYERS - 1)
    next_grad = arrange_group(gathered, next_index, feat_count, sub_count)
    next_grad = jnp.where(layer_group + 1 < LAYERS, next_grad, jnp.zeros_like(next_grad))
    recon_grads = jnp.stack([own_grad, next_grad], 0)
    feature_grad = jnp.einsum(
        "ktd,kfd->tf", recon_grads, dec_weight, preferred_element_type=jnp.float32
    )
    preact_grad = jnp.where(pre_act > 0.0, feature_grad, 0.0).astype(jnp.bfloat16)
    dec_grad = jnp.einsum(
        "tf,ktd->kfd", features, recon_grads, preferred_element_type=jnp.float32
    ).astype(jnp.bfloat16)
    enc_grad = lax.dot_general(
        inputs, preact_grad, (((0,), (0,)), ((), ())), preferred_element_type=jnp.float32
    ).astype(jnp.bfloat16)
    bias_grad = jnp.sum(preact_grad.astype(jnp.float32), 0)
    return (recon_error, mean_square, enc_grad, bias_grad, dec_grad)


def solution(mesh):
    placed = (
        P("feat", "layer"),
        P("feat", "layer"),
        P(None, ("layer", "feat")),
        P(("layer", "feat")),
        P(None, ("layer", "feat"), None),
    )
    return jax.shard_map(
        on_device,
        mesh=mesh,
        in_specs=placed,
        out_specs=(
            P("feat", "layer"),
            P(),
            P(None, ("layer", "feat")),
            P(("layer", "feat")),
            P(None, ("layer", "feat"), None),
        ),
        check_vma=False,
    )
```

profile of v0, /device:TPU:1, one launch (start us, length us, event | category | flops | bytes accessed | tf_op | source)
XLA Modules:
  0.0 725.6 jit_solution(8421036581591228015)
XLA Ops:
  7.2 0.0 all-gather.6.cloned.1.call-start
  7.2 1.5 collective-permute-start
  8.7 1.1 collective-permute-done
  9.7 0.8 broadcast_select_fusion.5
  10.5 3.8 collective-permute-start.1
  14.3 2.1 collective-permute-done.1
  16.5 1.4 collective-permute-start.2
  17.9 2.8 collective-permute-done.2
  20.7 0.7 pad_maximum_fusion
  21.5 0.0 all-gather.6.cloned.1.call-update
  21.5 0.0 copy-start.4
  21.5 0.0 all-reduce.2.cloned.1.call-start
  21.5 52.6 %all-gather.6.cloned.1.call-done = bf16[512,2048]{1,0:T(8,128)(2,1)} async-done(((bf16[64,2048]{1,0:T(8,128)(2,1)}), bf16[512,2048]{1,0:T(8,128)(2,1)}) %all-gather.6.cloned.1.call-update) | async-done | bytes 2097168 | tf_op jit(solution)/shard_map/all_gather | solution.py:50
  74.2 5.1 fusion.7
  79.3 0.0 copy-start.5
  79.3 1.3 copy-done.5
  80.7 0.0 copy-done.4
  80.7 9.4 %convolution_convert_fusion = bf16[512,2,2048]{2,0,1:T(8,128)(2,1)} fusion(bf16[2,1024,2048]{2,1,0:T(8,128)(2,1)} %param.9, f32[512,1024]{1,0:T(8,128)S(1)} %fusion.7, f32[1024]{0:T(1024)S(1)} %copy-done.4), kind=kOutput, calls=%fused_computation.1 | convolution fusion | flops 4298637312 | bytes 14684160 | tf_op jit(solution)/shard_map/tf,kfd->tkd/dot_general | solution.py:53
  90.1 0.0 all-reduce.2.cloned.1.call-update
  90.1 0.0 all-gather.8.cloned.1.call-start
  90.2 184.6 %all-reduce.2.cloned.1.call-done = bf16[512,2,2048]{2,0,1:T(8,128)(2,1)} async-done(((bf16[512,2,2048]{2,0,1:T(8,128)(2,1)}), bf16[512,2,2048]{2,0,1:T(8,128)(2,1)}) %all-reduce.2.cloned.1.call-update) | async-done | bytes 4194320 | tf_op jit(solution)/shard_map/psum | solution.py:56
  274.8 1.9 convert_convert_fusion
  276.7 0.0 all-gather.8.cloned.1.call-update
  276.7 0.0 all-gather.10.cloned.1.call-start
  276.8 0.0 copy-start.2
  276.9 75.4 %all-gather.8.cloned.1.call-done = bf16[1024,2,2048]{2,0,1:T(8,128)(2,1)} async-done(((bf16[64,2,2048]{2,0,1:T(8,128)(2,1)}), bf16[1024,2,2048]{2,0,1:T(8,128)(2,1)}) %all-gather.8.cloned.1.call-update) | async-done | bytes 8388624 | tf_op jit(solution)/shard_map/all_gather | solution.py:58
  352.2 11.3 %bitcast_convert_fusion = f32[16,64,2,2048]{3,1,0,2:T(8,128)} fusion(bf16[1024,2,2048]{2,0,1:T(8,128)(2,1)} %all-gather.8.cloned.1.call-done), kind=kLoop, calls=%fused_computation.30 | loop fusion | flops 4194304 | bytes 25165824 | tf_op jit(solution)/shard_map/convert_element_type | solution.py:60
  363.5 1.7 dynamic-slice_reduce_fusion
  365.2 0.0 copy-done.2
  365.2 0.6 multiply_convert_fusion
  365.9 0.0 copy-start.1
  365.9 0.0 all-gather.10.cloned.1.call-update
  365.9 0.6 multiply_reduce_fusion
  366.5 64.1 %psum.15 = f32[]{:T(128)} all-reduce(f32[]{:T(128)} %multiply_reduce_fusion), channel_id=1, replica_groups=mesh['layer'=16,'feat'=8] {'layer','feat'}, use_global_device_ids=true, to_apply=%region_4.5 | all-reduce | flops 1 | bytes 8 | tf_op jit(solution)/shard_map/psum | solution.py:73
  431.3 238.1 %all-gather.10.cloned.1.call-done = bf16[8192,256]{1,0:T(8,128)(2,1)} async-done(((bf16[64,256]{1,0:T(8,128)(2,1)}), bf16[8192,256]{1,0:T(8,128)(2,1)}) %all-gather.10.cloned.1.call-update) | async-done | bytes 4194320 | tf_op jit(solution)/shard_map/all_gather | solution.py:76
  669.4 2.7 constant_dynamic-slice_fusion
  672.1 0.0 copy-done.1
  672.1 4.4 fusion
  676.5 2.9 stack_reshape.3
  679.4 1.5 constant_dynamic-update-slice_fusion.1
  680.8 3.1 select_n.126
  683.9 0.0 slice-start
  683.9 1.5 constant_dynamic-update-slice_fusion
  685.3 0.0 copy-start
  685.3 0.0 slice-start.1
  685.4 0.0 copy-start.6
  685.4 11.2 %convert_bitcast_fusion = bf16[2,1024,2048]{1,2,0:T(8,128)(2,1)} fusion(bf16[2,512,2048]{2,1,0:T(8,128)(2,1)} %constant_dynamic-update-slice_fusion, f32[512,1024]{1,0:T(8,128)} %copy-done.5, f32[1024]{0:T(1024)S(1)} %copy-done.4), kind=kOutput, calls=%fused_computation | convolution fusion | flops 4300734464 | bytes 14684160 | tf_op jit(solution)/shard_map/tf,ktd->kfd/dot_general | solution.py:86
  696.6 0.0 slice-done
  696.6 0.0 copy-done
  696.6 0.0 slice-done.1
  696.6 0.0 copy-done.6
  696.6 5.2 convert_reduce_fusion
  701.8 0.0 copy-start.3
  701.8 11.7 %copy.13 = bf16[2,1024,2048]{2,1,0:T(8,128)(2,1)} copy(bf16[2,1024,2048]{1,2,0:T(8,128)(2,1)} %convert_bitcast_fusion) | data formatting | bytes 16777216
  713.6 0.0 copy-done.3
  713.6 4.4 convolution_convert_fusion.1
  (5 shorter events, 0.1 us)
Async XLA Ops:
  7.2 67.0 %all-gather.6.cloned.1.call-start = ((), (), s32[]{:S(2)}) async-start(), calls=%async_computation | async-start | bytes 2359296 | tf_op jit(solution)/shard_map/all_gather | solution.py:50
  7.2 2.5 collective-permute-start
  10.5 5.9 collective-permute-start.1
  16.5 4.2 collective-permute-start.2
  21.5 59.2 %copy-start.4 = (f32[1024]{0:T(1024)S(1)}, f32[1024]{0:T(1024)}, u32[]{:S(2)}) copy-start(f32[1024]{0:T(1024)} %param.8) | copy-start | bytes 12292
  21.5 253.3 %all-reduce.2.cloned.1.call-start = ((), (), s32[]{:S(2)}) async-start(), calls=%async_computation.1 | async-start | bytes 8388608 | tf_op jit(solution)/shard_map/psum | solution.py:56
  79.3 1.3 copy-start.5
  90.1 262.1 %all-gather.8.cloned.1.call-start = ((), (), s32[]{:S(2)}) async-start(), calls=%async_computation.2 | async-start | bytes 8912896 | tf_op jit(solution)/shard_map/all_gather | solution.py:58
  276.7 392.6 %all-gather.10.cloned.1.call-start = ((), (), s32[]{:S(2)}) async-start(), calls=%async_computation.3 | async-start | bytes 4227072 | tf_op jit(solution)/shard_map/all_gather | solution.py:76
  276.8 88.4 %copy-start.2 = (bf16[64,256]{1,0:T(8,128)(2,1)S(1)}, bf16[64,256]{1,0:T(8,128)(2,1)}, u32[]{:S(2)}) copy-start(bf16[64,256]{1,0:T(8,128)(2,1)} %param.6) | copy-start | bytes 98308
  365.9 306.2 %copy-start.1 = (f32[64,256]{1,0:T(8,128)}, f32[64,256]{1,0:T(8,128)S(1)}, u32[]{:S(2)}) copy-start(f32[64,256]{1,0:T(8,128)S(1)} %get-tuple-element.13) | copy-start | bytes 196612
  683.9 12.7 %slice-start = ((s8[8388608]{0:T(1024)(128)(4,1)}), s8[4194304]{0:T(1024)(128)(4,1)S(1)}, s32[]{:S(2)}) async-start(s8[8388608]{0:T(1024)(128)(4,1)} %bitcast.31), calls=%async_computation.4 | async-start | bytes 8388608
  685.3 11.2 %copy-start = (bf16[2,512,2048]{2,1,0:T(8,128)(2,1)S(1)}, bf16[2,512,2048]{2,1,0:T(8,128)(2,1)}, u32[]{:S(2)}) copy-start(bf16[2,512,2048]{2,1,0:T(8,128)(2,1)} %constant_dynamic-update-slice_fusion) | copy-start | bytes 12582916
  685.3 11.2 %slice-start.1 = ((s8[8388608]{0:T(1024)(128)(4,1)}), s8[4194304]{0:T(1024)(128)(4,1)S(1)}, s32[]{:S(2)}) async-start(s8[8388608]{0:T(1024)(128)(4,1)} %bitcast.31), calls=%async_computation.5 | async-start | bytes 8388608
  685.4 11.2 %copy-start.6 = (f32[512,1024]{1,0:T(8,128)S(1)}, f32[512,1024]{1,0:T(8,128)}, u32[]{:S(2)}) copy-start(f32[512,1024]{1,0:T(8,128)} %copy-done.5) | copy-start | bytes 6291460
  701.8 11.7 %copy-start.3 = (bf16[512,2048]{1,0:T(8,128)(2,1)S(1)}, bf16[512,2048]{1,0:T(8,128)(2,1)}, u32[]{:S(2)}) copy-start(bf16[512,2048]{1,0:T(8,128)(2,1)} %all-gather.6.cloned.1.call-done) | copy-start | bytes 6291460
Sparse Core Ops, SparseCore 0:
  21.6 52.5 all-gather.5
  90.3 184.5 all-reduce.1
  277.9 74.3 all-gather.7
  366.0 303.3 all-gather.9
where the time goes:
time: 726 us
  waiting for transfers between devices  557 us (77%)
  blocking collectives  64.1 us (9%)
  matrix products  35.4 us (5%)
  local copies, waits for them, and re-layouts  24.7 us (3%)
  other arithmetic  22 us (3%)
  between operations  15.7 us (2%)
    all_gather x1, waiting for transfers between devices, on_device(): lax.all_gather(scaled[None], ('layer', 'feat'), axis=0, tiled=True)  238 us
    psum x1, waiting for transfers between devices, on_device(): lax.psum(partial_value.astype(jnp.bfloat16), 'feat').astype(jnp.float32)  185 us
    all_gather x1, waiting for transfers between devices, on_device(): lax.all_gather(summed_rows[None].astype(jnp.bfloat16), 'layer', axis=0, t...  75.4 us
    psum x1, blocking collectives, on_device(): squares = lax.psum(jnp.sum(recon_error * recon_error), ('layer', 'feat'))  64.1 us
    all_gather x1, waiting for transfers between devices, on_device(): inputs = lax.all_gather(joined, 'feat', axis=0, tiled=True)  52.6 us
    unnamed x20, local copies, waits for them, and re-layouts  14.6 us
  transfers between devices with their start and end apart: 7, of which 7 were waited for; matrix products, arithmetic and copies ran while one was open for 0% of the time, Pallas kernels for 0%

commit v1 on v0

v1 whole, which is shorter than its diff:
```python
import jax
import jax.numpy as jnp
from jax import lax
from jax.experimental import pallas as pl
from jax.experimental.pallas import tpu as pltpu
from jax.sharding import PartitionSpec as P

D = 2048
LAYERS = 2
TOK = 512
SHARD = 1024
ROWS = 64
COLS = 256
LOSS_SCALE = 64.0
MESH = pl.DeviceIdType.MESH
BF16 = jnp.bfloat16
F32 = jnp.float32


def place(x, y, z, core):
    return (y * 4 + lax.div(z, 2) * 2 + core, x * 2 + lax.rem(z, 2))


def block_at(core, z, x):
    return z * (1 - core) + x * core, x * (1 - core) + z * core


def column_block(ref, lead, y, z_high, core):
    pieces = []
    for x in range(4):
        for z_low in range(2):
            big, small = block_at(core, z_high * 2 + z_low, x)
            pieces.append(ref[(*lead, y, core, big, small)])
    return jnp.concatenate(pieces, 0)


def all_columns(ref, lead):
    return jnp.concatenate(
        [column_block(ref, lead, m // 4, m // 2 % 2, m % 2) for m in range(8)], 1
    )


def add_into(ref, other):
    ref[...] = (ref[...].astype(F32) + other[...].astype(F32)).astype(BF16)


K_TOK_Y = 0
K_TOK = 1
K_PART = 14
K_RS_BIG = 16
K_RS_SMALL = 28
K_RS_Y = 40
K_CROSS = 42
K_S_Y = 43
K_S_CROSS = 44
K_S_FWD = 45
K_S = 46
K_MS = 72
K_COUNT = 79


def step_kernel(
    tok, tgt, enc, bias, dec,
    rerr, msq, gt_out, ft_out, s_out, pg_out, bg,
    encv, decv, g, pre, feat, p, rc, big_in, r1, small_in, r2, y_in, cross_in, cross_out,
    total, s, fg, gt, ft, pg, ms_in, ms_own, send_sem, recv_sem, local_sem,
):
    me_layer = lax.axis_index("layer")
    me_feat = lax.axis_index("feat")
    core = lax.rem(me_layer, 2)
    y = lax.div(me_layer, 4)
    x = lax.div(me_feat, 2)
    z = lax.rem(lax.div(me_layer, 2), 2) * 2 + lax.rem(me_feat, 2)
    yb = lax.rem(y, 2)
    first_layer = y < 2
    second_layer = y >= 2

    partner = place(x, y, z, 1 - core)
    y_pair = place(x, y + 1 - 2 * yb, z, core)
    y_cross = place(x, 3 - y, z, core)
    x_right, x_left = lax.rem(x + 1, 4), lax.rem(x + 3, 4)
    z_right, z_left = lax.rem(z + 1, 4), lax.rem(z + 3, 4)

    def big_place(step):
        return place(
            lax.rem(x + core * step, 4), y, lax.rem(z + (1 - core) * step, 4), core
        )

    def small_place(step):
        return place(
            lax.rem(x + (1 - core) * step, 4), y, lax.rem(z + core * step, 4), core
        )

    big_pos, small_pos = block_at(core, z, x)
    big_ring = (big_pos, big_place(1), big_place(3))
    small_ring = (small_pos, small_place(1), small_place(3))

    pending = []

    def send(src, dst, number, device):
        return pltpu.make_async_remote_copy(
            src_ref=src,
            dst_ref=dst,
            send_sem=send_sem.at[number],
            recv_sem=recv_sem.at[number],
            device_id=device,
            device_id_type=MESH,
        )

    enc_copy = pltpu.make_async_copy(enc, encv, local_sem.at[0])
    dec_copy = pltpu.make_async_copy(dec, decv, local_sem.at[1])
    enc_copy.start()
    dec_copy.start()

    barrier = pltpu.get_barrier_semaphore()
    for device in (
        partner,
        y_pair,
        y_cross,
        place(x_right, y, z, core),
        place(x_left, y, z, core),
        place(x, y, z_right, core),
        place(x, y, z_left, core),
    ):
        pl.semaphore_signal(barrier, inc=1, device_id=device, device_id_type=MESH)
    pl.semaphore_wait(barrier, 7)

    def ring_copies(ref_of, ring, number):
        pos, right, left = ring
        own = ref_of(slice(None), pos)
        from_left = ref_of(0, lax.rem(pos + 3, 4))
        from_right = ref_of(1, lax.rem(pos + 1, 4))
        return (
            send(own, own, number, right),
            send(own, own, number + 1, left),
            send(from_left, from_left, number + 2, right),
            send(from_right, from_right, number + 3, left),
        )

    def gather_pieces(buf, t, number):
        small = ring_copies(
            lambda half, i: buf.at[t, half, core, big_pos, i], small_ring, number
        )
        large = ring_copies(lambda half, i: buf.at[t, half, core, i], big_ring, number + 4)
        whole = slice(None)
        opposite = lax.rem(big_pos + 2, 4)
        shared = []
        for half, i in (
            (whole, big_pos),
            (whole, lax.rem(big_pos + 3, 4)),
            (whole, lax.rem(big_pos + 1, 4)),
            (0, opposite),
            (1, opposite),
        ):
            ref = buf.at[t, half, core, i]
            shared.append(send(ref, ref, number + 8 + len(shared), partner))

        class Pieces:
            def small_start(self):
                small[0].start()
                small[1].start()

            def small_mid(self):
                small[0].wait_recv()
                small[2].start()
                small[1].wait_recv()
                small[3].start()

            def small_end(self):
                small[2].wait_recv()
                small[3].wait_recv()

            def big_start(self):
                large[0].start()
                large[1].start()
                shared[0].start()

            def big_mid(self):
                large[0].wait_recv()
                large[2].start()
                large[1].wait_recv()
                large[3].start()
                shared[1].start()
                shared[2].start()

            def big_end(self):
                large[2].wait_recv()
                shared[3].start()
                large[3].wait_recv()
                shared[4].start()

            def shared_end(self):
                for copy in shared:
                    copy.wait_recv()

            def drain(self):
                for copy in (*small, *large, *shared):
                    copy.wait_send()

        return Pieces()

    g[0, yb, core, big_pos, small_pos] = tok[...]
    own = g.at[0, yb, core, big_pos, small_pos]
    tok_y = send(own, own, K_TOK_Y, y_pair)
    tok_y.start()
    tok_y.wait_recv()
    tokens = gather_pieces(g, 0, K_TOK)
    tokens.small_start()
    tokens.small_mid()
    tokens.small_end()
    tokens.big_start()
    tokens.big_mid()
    tokens.big_end()
    tokens.shared_end()

    enc_copy.wait()

    @pl.loop(0, 4)
    def _(n):
        cols = pl.ds(pl.multiple_of(n * 256, 256), 256)
        act = (
            jnp.dot(all_columns(g, (0,)), encv[:, cols], preferred_element_type=F32)
            + bias[:, cols]
        )
        pre[:, cols] = act
        feat[:, cols] = jnp.maximum(act, 0.0).astype(BF16)

    dec_copy.wait()

    def decode(t, to_core):
        @pl.loop(0, 4)
        def _(i):
            to_y, z_high = lax.div(i, 2), lax.rem(i, 2)
            first = pl.multiple_of((to_y * 4 + z_high * 2 + to_core) * 256, 256)
            value = jnp.dot(
                feat[...], decv[t, :, pl.ds(first, 256)], preferred_element_type=F32
            ).astype(BF16)
            for to_x in range(4):
                for z_low in range(2):
                    big, small = block_at(to_core, z_high * 2 + z_low, to_x)
                    at = (to_x * 2 + z_low) * ROWS
                    p[t, to_y, to_core, big, small] = value[at : at + ROWS]

    def part_copy(t):
        return send(p.at[t, :, 1 - core], rc.at[t], K_PART + t, partner)

    def part_add(t):
        part_copy(t).wait_recv()

        @pl.loop(0, 8)
        def _(i):
            h, b = lax.div(i, 4), lax.rem(i, 4)
            add_into(p.at[t, h, core, b], rc.at[t, h, b])

    def scatter_pieces(q, bufs, ring, number):
        pos, right, left = ring
        at_right, at_left, opposite = (
            lax.rem(pos + 1, 4),
            lax.rem(pos + 3, 4),
            lax.rem(pos + 2, 4),
        )
        copies = (
            send(q(0, opposite), bufs(0), number, right),
            send(q(1, opposite), bufs(1), number + 1, left),
            send(q(1, at_right), bufs(2), number + 2, right),
            send(q(0, at_left), bufs(3), number + 3, left),
            send(q(0, at_right), bufs(4), number + 4, right),
            send(q(1, at_left), bufs(5), number + 5, left),
        )

        class Pieces:
            def start(self):
                for copy in copies[:4]:
                    copy.start()

            def mid(self):
                copies[0].wait_recv()
                add_into(q(0, at_right), bufs(0))
                copies[4].start()
                copies[1].wait_recv()
                add_into(q(1, at_left), bufs(1))
                copies[5].start()

            def end(self, out):
                copies[3].wait_recv()
                copies[4].wait_recv()
                out[0] = (
                    q(0, pos)[...].astype(F32)
                    + bufs(3)[...].astype(F32)
                    + bufs(4)[...].astype(F32)
                ).astype(BF16)
                copies[2].wait_recv()
                copies[5].wait_recv()
                out[1] = (
                    q(1, pos)[...].astype(F32)
                    + bufs(2)[...].astype(F32)
                    + bufs(5)[...].astype(F32)
                ).astype(BF16)

            def drain(self):
                for copy in copies:
                    copy.wait_send()

        return Pieces()

    def big_scatter(t):
        return scatter_pieces(
            lambda h, i: p.at[t, h, core, i],
            lambda k: big_in.at[t, k],
            big_ring,
            K_RS_BIG + 6 * t,
        )

    def small_scatter(t):
        return scatter_pieces(
            lambda h, i: r1.at[t, h, i],
            lambda k: small_in.at[t, k],
            small_ring,
            K_RS_SMALL + 6 * t,
        )

    def y_copy(t):
        away = 1 - yb if t == 0 else yb
        return send(r2.at[t, away], y_in.at[t], K_RS_Y + t, y_pair)

    def cross_copy():
        return send(cross_out, cross_in, K_CROSS, y_cross)

    def part(t):
        decode(t, 1 - core)
        part_copy(t).start()

    @pl.when(first_layer)
    def _():
        part(1)
        decode(1, core)
        part_add(1)
        big_scatter(1).start()

    part(0)

    @pl.when(first_layer)
    def _():
        big_scatter(1).mid()

    decode(0, core)
    part_add(0)
    big_scatter(0).start()

    @pl.when(first_layer)
    def _():
        big_scatter(1).end(r1.at[1])
        small_scatter(1).start()

    big_scatter(0).mid()

    @pl.when(first_layer)
    def _():
        small_scatter(1).mid()

    big_scatter(0).end(r1.at[0])
    small_scatter(0).start()

    @pl.when(first_layer)
    def _():
        small_scatter(1).end(r2.at[1])
        y_copy(1).start()

    small_scatter(0).mid()

    @pl.when(first_layer)
    def _():
        y_copy(1).wait_recv()
        cross_out[...] = (
            r2[1, 1 - yb].astype(F32) + y_in[1].astype(F32)
        ).astype(BF16)
        cross_copy().start()

    small_scatter(0).end(r2.at[0])
    y_copy(0).start()
    y_copy(0).wait_recv()
    total[...] = r2[0, yb].astype(F32) + y_in[0].astype(F32)

    @pl.when(second_layer)
    def _():
        cross_copy().wait_recv()
        total[...] = total[...] + cross_in[...].astype(F32)

    error = total[...] - tgt[...].astype(F32)
    rerr[...] = error
    s[0, yb, core, big_pos, small_pos] = (LOSS_SCALE / TOK * error).astype(BF16)
    own_s = s.at[0, yb, core, big_pos, small_pos]
    s_y = send(own_s, own_s, K_S_Y, y_pair)
    s_y.start()
    s_cross = send(own_s, s.at[1, yb, core, big_pos, small_pos], K_S_CROSS, y_cross)

    @pl.when(second_layer)
    def _():
        s_cross.start()

    squares = error * error
    tile = jnp.zeros((8, 128), F32)
    for i in range(8):
        for j in range(2):
            tile = tile + squares[i * 8 : i * 8 + 8, j * 128 : j * 128 + 128]
    ms_own[0] = tile

    ms_places = (
        partner,
        place(x + 1 - 2 * lax.rem(x, 2), y, z, core),
        place(3 - x, y, z, core),
        place(x, y, z + 1 - 2 * lax.rem(z, 2), core),
        place(x, y, 3 - z, core),
        y_pair,
        y_cross,
    )

    def ms_copy(i):
        return send(ms_own.at[i], ms_in.at[i], K_MS + i, ms_places[i])

    def ms_step(i):
        ms_copy(i).wait_recv()
        ms_own[i + 1] = ms_own[i] + ms_in[i]
        if i < 6:
            ms_copy(i + 1).start()

    ms_copy(0).start()

    def feature_grad(t, n):
        rows = pl.ds(pl.multiple_of(n * 256, 256), 256)
        value = lax.dot_general(
            all_columns(s, (t,)),
            decv[t, rows, :],
            (((1,), (1,)), ((), ())),
            preferred_element_type=F32,
        )
        if t == 0:
            fg[:, rows] = value
        else:
            fg[:, rows] = fg[:, rows] + value

    s0 = gather_pieces(s, 0, K_S)
    s1 = gather_pieces(s, 1, K_S + 13)
    got = s.at[1, 1 - yb, core, big_pos, small_pos]
    s_fwd = send(got, got, K_S_FWD, y_pair)

    s_y.wait_recv()
    s0.small_start()

    @pl.when(first_layer)
    def _():
        s_cross.wait_recv()
        s_fwd.start()

    ms_step(0)
    s0.small_mid()

    @pl.when(first_layer)
    def _():
        s_fwd.wait_recv()
        s1.small_start()

    ms_step(1)
    s0.small_end()
    s0.big_start()
    ms_step(2)

    @pl.when(first_layer)
    def _():
        s1.small_mid()

    ms_step(3)

    @pl.when(first_layer)
    def _():
        s1.small_end()
        s1.big_start()

    ms_step(4)
    s0.big_mid()
    ms_step(5)
    s0.big_end()
    s0.shared_end()
    s_store0 = pltpu.make_async_copy(s.at[0], s_out.at[0], local_sem.at[2])
    s_store0.start()
    ms_step(6)
    msq[0, 0] = jnp.sum(ms_own[7]) / (LAYERS * TOK * D)

    @pl.loop(0, 2)
    def _(n):
        feature_grad(0, n)

    @pl.when(first_layer)
    def _():
        s1.big_mid()

    @pl.loop(2, 4)
    def _(n):
        feature_grad(0, n)

    s_store1 = pltpu.make_async_copy(s.at[1], s_out.at[1], local_sem.at[3])

    @pl.when(first_layer)
    def _():
        s1.big_end()
        s1.shared_end()
        s_store1.start()

        @pl.loop(0, 4)
        def _(n):
            feature_grad(1, n)

    @pl.loop(0, 4)
    def _(n):
        cols = pl.ds(pl.multiple_of(n * 256, 256), 256)
        grad = jnp.where(pre[:, cols] > 0.0, fg[:, cols], 0.0).astype(BF16)
        pg[:, cols] = grad
        bg[:, cols] = jnp.sum(grad.astype(F32), 0, keepdims=True)

    pg_store = pltpu.make_async_copy(pg, pg_out, local_sem.at[4])
    pg_store.start()

    @pl.loop(0, 4)
    def _(n):
        cols = pl.ds(pl.multiple_of(n * 256, 256), 256)
        ft[cols, :] = feat[:, cols].T

    ft_store = pltpu.make_async_copy(ft, ft_out, local_sem.at[5])
    ft_store.start()

    @pl.loop(0, 8)
    def _(m):
        block = column_block(g, (0,), lax.div(m, 4), lax.rem(lax.div(m, 2), 2), lax.rem(m, 2))
        gt[pl.ds(pl.multiple_of(m * 256, 256), 256), :] = block.T

    gt_store = pltpu.make_async_copy(gt, gt_out, local_sem.at[6])
    gt_store.start()

    tok_y.wait_send()
    tokens.drain()
    part_copy(0).wait_send()
    big_scatter(0).drain()
    small_scatter(0).drain()
    y_copy(0).wait_send()
    s_y.wait_send()
    s0.drain()
    for i in range(7):
        ms_copy(i).wait_send()

    @pl.when(first_layer)
    def _():
        part_copy(1).wait_send()
        big_scatter(1).drain()
        small_scatter(1).drain()
        y_copy(1).wait_send()
        cross_copy().wait_send()
        s_fwd.wait_send()
        s1.drain()
        s_store1.wait()

    @pl.when(second_layer)
    def _():
        s_cross.wait_send()

    s_store0.wait()
    pg_store.wait()
    ft_store.wait()
    gt_store.wait()


def weight_grads_kernel(gt, ft, s, pg, dec_grad, enc_grad):
    i = pl.program_id(0)
    first_layer = lax.axis_index("layer") < 8

    def dec_block(t):
        m = i - 8 * t
        block = column_block(
            s, (t,), lax.div(m, 4), lax.rem(lax.div(m, 2), 2), lax.rem(m, 2)
        )
        dec_grad[0] = jnp.dot(ft[...], block, preferred_element_type=F32).astype(BF16)

    @pl.when(i < 8)
    def _():
        dec_block(0)

    @pl.when((i >= 8) & (i < 16) & first_layer)
    def _():
        dec_block(1)

    @pl.when((i >= 8) & (i < 16) & jnp.logical_not(first_layer))
    def _():
        dec_grad[...] = jnp.zeros_like(dec_grad)

    @pl.when(i >= 16)
    def _():
        rows = pl.ds(pl.multiple_of((i - 16) * 256, 256), 256)
        enc_grad[...] = jnp.dot(
            gt[rows, :], pg[...], preferred_element_type=F32
        ).astype(BF16)


def on_device(tokens_in, targets, enc_weight, enc_bias, dec_weight):
    vmem = pl.BlockSpec(memory_space=pltpu.VMEM)
    anywhere = pl.BlockSpec(memory_space=pl.ANY)
    shape = jax.ShapeDtypeStruct
    blocks = (2, 2, 4, 4, ROWS, COLS)
    rerr, msq, gt, ft, s, pg, bg = pl.pallas_call(
        step_kernel,
        out_shape=(
            shape((ROWS, COLS), F32),
            shape((1, 1), F32),
            shape((D, TOK), BF16),
            shape((SHARD, TOK), BF16),
            shape((2, *blocks), BF16),
            shape((TOK, SHARD), BF16),
            shape((1, SHARD), F32),
        ),
        in_specs=[vmem, vmem, anywhere, vmem, anywhere],
        out_specs=(
            vmem,
            pl.BlockSpec(memory_space=pltpu.SMEM),
            anywhere,
            anywhere,
            anywhere,
            anywhere,
            vmem,
        ),
        scratch_shapes=[
            pltpu.VMEM((D, SHARD), BF16),
            pltpu.VMEM((2, SHARD, D), BF16),
            pltpu.VMEM((1, *blocks), BF16),
            pltpu.VMEM((TOK, SHARD), F32),
            pltpu.VMEM((TOK, SHARD), BF16),
            pltpu.VMEM((2, *blocks), BF16),
            pltpu.VMEM((2, 2, 4, 4, ROWS, COLS), BF16),
            pltpu.VMEM((2, 6, 4, ROWS, COLS), BF16),
            pltpu.VMEM((2, 2, 4, ROWS, COLS), BF16),
            pltpu.VMEM((2, 6, ROWS, COLS), BF16),
            pltpu.VMEM((2, 2, ROWS, COLS), BF16),
            pltpu.VMEM((2, ROWS, COLS), BF16),
            pltpu.VMEM((ROWS, COLS), BF16),
            pltpu.VMEM((ROWS, COLS), BF16),
            pltpu.VMEM((ROWS, COLS), F32),
            pltpu.VMEM((2, *blocks), BF16),
            pltpu.VMEM((TOK, SHARD), F32),
            pltpu.VMEM((D, TOK), BF16),
            pltpu.VMEM((SHARD, TOK), BF16),
            pltpu.VMEM((TOK, SHARD), BF16),
            pltpu.VMEM((7, 8, 128), F32),
            pltpu.VMEM((8, 8, 128), F32),
            pltpu.SemaphoreType.DMA((K_COUNT,)),
            pltpu.SemaphoreType.DMA((K_COUNT,)),
            pltpu.SemaphoreType.DMA((7,)),
        ],
        compiler_params=pltpu.CompilerParams(
            collective_id=0, has_side_effects=True, vmem_limit_bytes=56 * 2**20
        ),
        name="step",
    )(tokens_in, targets, enc_weight, enc_bias.reshape(1, SHARD), dec_weight)

    dec_grad, enc_grad = pl.pallas_call(
        weight_grads_kernel,
        grid=(24,),
        out_shape=(shape((2, SHARD, D), BF16), shape((D, SHARD), BF16)),
        in_specs=[vmem] * 4,
        out_specs=(
            pl.BlockSpec(
                (1, SHARD, 256),
                lambda i: (jnp.minimum(i, 15) // 8, 0, jnp.minimum(i, 15) % 8),
            ),
            pl.BlockSpec((256, SHARD), lambda i: (jnp.maximum(i - 16, 0), 0)),
        ),
        compiler_params=pltpu.CompilerParams(vmem_limit_bytes=40 * 2**20),
        name="weight_grads",
    )(gt, ft, s, pg)
    return (rerr, msq.reshape(()), enc_grad, bg.reshape(SHARD), dec_grad)


def solution(mesh):
    placed = (
        P("feat", "layer"),
        P("feat", "layer"),
        P(None, ("layer", "feat")),
        P(("layer", "feat")),
        P(None, ("layer", "feat"), None),
    )
    return jax.shard_map(
        on_device,
        mesh=mesh,
        in_specs=placed,
        out_specs=(
            P("feat", "layer"),
            P(),
            P(None, ("layer", "feat")),
            P(("layer", "feat")),
            P(None, ("layer", "feat"), None),
        ),
        check_vma=False,
    )
```

time: 726 us -> 128 us (0.18)
  waiting for transfers between devices: 557 us -> 0 us
  Pallas kernels: 0 us -> 117 us
  blocking collectives: 64.1 us -> 0 us
  matrix products: 35.4 us -> 0 us
  other arithmetic: 22 us -> 0 us
  local copies, waits for them, and re-layouts: 24.7 us -> 7.45 us
  between operations: 15.7 us -> 2.49 us
    all_gather x3 -> x0, waiting for transfers between devices: 366 us -> none  [the longest x1 238 us: on_device(): lax.all_gather(scaled[None], ('layer', 'feat'), axis=0, tiled=True)]
    psum x1 -> x0, waiting for transfers between devices: 185 us -> none  [on_device(): lax.psum(partial_value.astype(jnp.bfloat16), 'feat').astype(jnp.float32)]
    pallas_call x0 -> x2, Pallas kernels: none -> 117 us  [the longest x1 102 us: on_device(): pl.pallas_call(step_kernel, out_shape=(shape((ROWS, COLS), F32), shape((1...]
    psum x1 -> x0, blocking collectives: 64.1 us -> none  [on_device(): squares = lax.psum(jnp.sum(recon_error * recon_error), ('layer', 'feat'))]
    dot_general x5 -> x0, matrix products: 35.4 us -> none  [the longest x1 11.2 us: on_device(): jnp.einsum('tf,ktd->kfd', features, recon_grads, preferred_element_type=j...]
    convert_element_type x3 -> x0, other arithmetic: 13.8 us -> none  [the longest x1 11.3 us: on_device(): gathered = lax.all_gather(summed_rows[None].astype(jnp.bfloat16), 'layer'...]
    unnamed x20 -> x14, local copies, waits for them, and re-layouts: 14.6 us -> 7.45 us
  transfers between devices with their start and end apart: 7 -> 0, of which waited for: 7 -> 0; matrix products, arithmetic and copies ran while one was open for 0% -> 0% of each run, Pallas kernels for 0% -> 0%
where the time goes in v1:
time: 128 us; the launch traced here: 127 us
  Pallas kernels  117 us (91%)
  local copies, waits for them, and re-layouts  7.45 us (6%)
  between operations  2.49 us (2%)
    pallas_call x1, Pallas kernels, on_device(): pl.pallas_call(step_kernel, out_shape=(shape((ROWS, COLS), F32), shape((1...  102 us
    pallas_call x1, Pallas kernels, on_device(): pl.pallas_call(weight_grads_kernel, grid=(24,), out_shape=(shape((2, SHAR...  15.6 us
    unnamed x14, local copies, waits for them, and re-layouts  7.45 us

profile of v1, /device:TPU:1, one launch (start us, length us, event | category | flops | bytes accessed | tf_op | source)
XLA Modules:
  0.0 127.2 jit_solution(7035270113712619220)
XLA Ops:
  0.6 101.7 %step.1 = (f32[64,256]{1,0:T(8,128)}, f32[1,1]{1,0:T(1,128)}, bf16[2048,512]{1,0:T(8,128)(2,1)}, bf16[1024,512]{1,0:T(8,128)(2,1)}, bf16[2,2,2,4,4,64,256]{6,5,4...) custom-call(bf16[64,256]{1,0:T(8,128)(2,1)} %tok.1, bf16[64,256]{1,0:T(8,128)(2,1)} %tgt.1, ...), custom_call_target="tpu_custom_call" | custom-call | tf_op jit(solution)/shard_map/step/pallas_call | solution.py:607
  102.3 0.0 copy-start
  102.3 2.2 %copy-done = bf16[2,2,2,4,4,64,256]{6,5,4,3,2,1,0:T(8,128)(2,1)S(1)} copy-done((bf16[2,2,2,4,4,64,256]{6,5,4,3,2,1,0:T(8,128)(2,1)S(1)}, bf16[2,2,2,4,4,64,256]{6,5,4,3,2,1,0:T(8,128)(2,1)}, u32[]{:S(2)}) %copy-start) | copy-done | bytes 4194328
  104.5 0.0 copy-start.1
  104.5 1.6 %copy-done.1 = bf16[2048,512]{1,0:T(8,128)(2,1)S(1)} copy-done((bf16[2048,512]{1,0:T(8,128)(2,1)S(1)}, bf16[2048,512]{1,0:T(8,128)(2,1)}, u32[]{:S(2)}) %copy-start.1) | copy-done | bytes 2097176
  106.1 0.0 copy-start.2
  106.1 1.2 copy-done.2
  107.3 0.0 copy-start.3
  107.3 1.2 copy-done.3
  108.5 0.0 copy-start.4
  108.5 0.0 copy-start.5
  108.5 15.6 %weight_grads.1 = (bf16[2,1024,2048]{2,1,0:T(8,128)(2,1)}, bf16[2048,1024]{1,0:T(8,128)(2,1)}) custom-call(bf16[2048,512]{1,0:T(8,128)(2,1)S(1)} %copy-done.1, bf16[1024,512]{1,0:T(8,128)(2,1)S(1)} %copy-done.2, bf16[2,2,2,4,4,64,256]{6,5,4,3,2,1,0:T(8,128)(2,1)S(1)} %copy-done, bf16[512,1024]{1,0:T(8,128)(2,1)S(1)} %copy-done.3), custom_call_target="tpu_custom_call" | custom-call | tf_op jit(solution)/shard_map/weight_grads/pallas_call | solution.py:661
  124.2 0.0 copy-done.4
  124.2 0.6 copy.13
  125.5 0.0 copy-done.5
  125.5 0.6 copy.15
Async XLA Ops:
  102.3 2.2 %copy-start = (bf16[2,2,2,4,4,64,256]{6,5,4,3,2,1,0:T(8,128)(2,1)S(1)}, bf16[2,2,2,4,4,64,256]{6,5,4,3,2,1,0:T(8,128)(2,1)}, u32[]{:S(2)}) copy-start(bf16[2,2,2,4,4,64,256]{6,5,4,3,2,1,0:T(8,128)(2,1)} %get-tuple-element.18.s) | copy-start | bytes 12582916
  104.5 1.6 %copy-start.1 = (bf16[2048,512]{1,0:T(8,128)(2,1)S(1)}, bf16[2048,512]{1,0:T(8,128)(2,1)}, u32[]{:S(2)}) copy-start(bf16[2048,512]{1,0:T(8,128)(2,1)} %get-tuple-element.16.gt) | copy-start | bytes 6291460
  106.1 1.2 copy-start.2
  107.3 1.2 copy-start.3
  108.5 15.6 %copy-start.4 = (f32[64,256]{1,0:T(8,128)S(1)}, f32[64,256]{1,0:T(8,128)}, u32[]{:S(2)}) copy-start(f32[64,256]{1,0:T(8,128)} %get-tuple-element.28) | copy-start | bytes 196612
  108.5 17.0 %copy-start.5 = (f32[1,1024]{1,0:T(1,128)S(1)}, f32[1,1024]{1,0:T(1,128)}, u32[]{:S(2)}) copy-start(f32[1,1024]{1,0:T(1,128)} %get-tuple-element.21) | copy-start | bytes 12292

commit v2 on v0

v2 whole, which is shorter than its diff:
```python
import jax
import jax.numpy as jnp
from jax import lax
from jax.experimental import pallas as pl
from jax.experimental.pallas import tpu as pltpu
from jax.sharding import PartitionSpec as P

D = 2048
LAYERS = 2
TOK = 512
SHARD = 1024
ROWS = 64
COLS = 256
LOSS_SCALE = 64.0
MESH = pl.DeviceIdType.MESH
BF16 = jnp.bfloat16
F32 = jnp.float32


def place(x, y, z, core):
    return (y * 4 + lax.div(z, 2) * 2 + core, x * 2 + lax.rem(z, 2))


def block_at(half, z, x):
    return z * (1 - half) + x * half, x * (1 - half) + z * half


def column_block(ref, lead, half, z_high, core):
    pieces = []
    for x in range(4):
        for z_low in range(2):
            big, small = block_at(half, z_high * 2 + z_low, x)
            pieces.append(ref[(*lead, half, core, big, small)])
    return jnp.concatenate(pieces, 0)


def all_columns(ref, lead):
    return jnp.concatenate(
        [column_block(ref, lead, m // 4, m // 2 % 2, m % 2) for m in range(8)], 1
    )


class Numbers:
    def __init__(self):
        self.count = 0

    def take(self, *dims):
        if not dims:
            self.count += 1
            return self.count - 1
        return [self.take(*dims[1:]) for _ in range(dims[0])]


NUMBERS = Numbers()
K_GATHER = [
    dict(
        y=NUMBERS.take(),
        small=NUMBERS.take(2, 4),
        big=NUMBERS.take(2, 4),
        shared=NUMBERS.take(2, 4),
    )
    for _ in range(3)
]
K_PART = NUMBERS.take(2, 2)
K_BIG = NUMBERS.take(2, 2, 4)
K_SMALL = NUMBERS.take(2, 2, 4)
K_Y = NUMBERS.take()
K_CROSS = NUMBERS.take(2)
K_BACK = NUMBERS.take(2)
K_SQUARE = NUMBERS.take(4, 4)
K_COUNT = NUMBERS.count


def step_kernel(
    tok, tgt, enc, bias, dec,
    rerr, msq, gt_out, ft_out, s_out, pg_out, bg,
    encv, decv, g, pre, feat, p, rc, big_in, r1, small_in, r2, y_in, cross_in,
    s, fg, gt, ft, pg, squares_in, squares_own, send_sem, recv_sem, local_sem,
):
    me_layer = lax.axis_index("layer")
    me_feat = lax.axis_index("feat")
    core = lax.rem(me_layer, 2)
    y = lax.div(me_layer, 4)
    x = lax.div(me_feat, 2)
    z = lax.rem(lax.div(me_layer, 2), 2) * 2 + lax.rem(me_feat, 2)
    yb = lax.rem(y, 2)
    first_layer = y < 2
    second_layer = y >= 2

    def turn(v, step):
        return lax.rem(v + step, 4)

    partner = place(x, y, z, 1 - core)
    y_pair = place(x, y + 1 - 2 * yb, z, core)
    x_peers = [None] + [place(turn(x, o), y, z, core) for o in (1, 2, 3)]
    y_peers = [None] + [place(x, turn(y, o), z, core) for o in (1, 2, 3)]
    z_peers = [None] + [place(x, y, turn(z, o), core) for o in (1, 2, 3)]
    big_pos, small_pos = (z, x), (x, z)
    big_peers, small_peers = (z_peers, x_peers), (x_peers, z_peers)
    HALVES = (0, 1)
    OFFSETS = (1, 3, 2)

    def send(src, dst, number, device):
        return pltpu.make_async_remote_copy(
            src_ref=src,
            dst_ref=dst,
            send_sem=send_sem.at[number],
            recv_sem=recv_sem.at[number],
            device_id=device,
            device_id_type=MESH,
        )

    sent = []
    sent_first = []

    def go(log, make, *args):
        make(*args).start()
        log.append((make, args))

    def drain(log):
        for make, args in log:
            make(*args).wait_send()

    enc_copy = pltpu.make_async_copy(enc, encv, local_sem.at[0])
    dec_copy = pltpu.make_async_copy(dec, decv, local_sem.at[1])
    enc_copy.start()
    dec_copy.start()

    barrier = pltpu.get_barrier_semaphore()
    for device in (partner, *x_peers[1:], *y_peers[1:], *z_peers[1:]):
        pl.semaphore_signal(barrier, inc=1, device_id=device, device_id_type=MESH)
    pl.semaphore_wait(barrier, 10)

    class Gather:
        def __init__(self, buf, t, numbers, log):
            self.buf, self.t, self.numbers, self.log = buf, t, numbers, log

        def piece(self, half):
            return self.buf.at[self.t, half, core, big_pos[half], small_pos[half]]

        def chunk(self, half, i):
            return self.buf.at[self.t, half, core, i]

        def small_copy(self, half, o):
            ref = self.piece(half)
            return send(ref, ref, self.numbers["small"][half][o], small_peers[half][o])

        def big_copy(self, half, o):
            ref = self.chunk(half, big_pos[half])
            return send(ref, ref, self.numbers["big"][half][o], big_peers[half][o])

        def shared_copy(self, half, o):
            ref = self.chunk(half, turn(big_pos[half], 4 - o))
            return send(ref, ref, self.numbers["shared"][half][o], partner)

        def small(self, half):
            for o in OFFSETS:
                go(self.log, self.small_copy, half, o)

        def big(self, half):
            for o in OFFSETS:
                self.small_copy(half, o).wait_recv()
            for o in OFFSETS:
                go(self.log, self.big_copy, half, o)
            go(self.log, self.shared_copy, half, 0)

        def share(self, half):
            for o in OFFSETS:
                self.big_copy(half, o).wait_recv()
                go(self.log, self.shared_copy, half, o)

        def done(self):
            for half in HALVES:
                for o in range(4):
                    self.shared_copy(half, o).wait_recv()

    def own_half(buf, value):
        big, small = block_at(yb, z, x)
        buf[0, yb, core, big, small] = value
        return buf.at[0, yb, core, big, small]

    def by_half(fn):
        @pl.when(yb == 0)
        def _():
            fn(0, 1)

        @pl.when(yb == 1)
        def _():
            fn(1, 0)

    own = own_half(g, tok[...])
    tok_y = send(own, own, K_GATHER[2]["y"], y_pair)
    go(sent, lambda: tok_y)
    unlogged = []

    def first_hops(gather, y_copy):
        def run(mine, other):
            gather.small(mine)
            y_copy.wait_recv()
            gather.small(other)

        return run

    tokens = Gather(g, 0, K_GATHER[2], unlogged)
    by_half(first_hops(tokens, tok_y))

    def big_hops(gather):
        def run(mine, other):
            gather.big(mine)
            gather.big(other)

        return run

    by_half(big_hops(tokens))

    def share_hops(gather):
        def run(mine, other):
            gather.share(mine)
            gather.share(other)

        return run

    by_half(share_hops(tokens))
    tokens.done()

    enc_copy.wait()

    @pl.loop(0, 4)
    def _(n):
        cols = pl.ds(pl.multiple_of(n * 256, 256), 256)
        act = (
            jnp.dot(all_columns(g, (0,)), encv[:, cols], preferred_element_type=F32)
            + bias[:, cols]
        )
        pre[:, cols] = act
        feat[:, cols] = jnp.maximum(act, 0.0).astype(BF16)

    dec_copy.wait()

    def decode(t, to_core, half):
        @pl.loop(0, 2)
        def _(z_high):
            first = pl.multiple_of((half * 4 + z_high * 2 + to_core) * 256, 256)
            value = jnp.dot(
                feat[...], decv[t, :, pl.ds(first, 256)], preferred_element_type=F32
            ).astype(BF16)
            for to_x in range(4):
                for z_low in range(2):
                    big, small = block_at(half, z_high * 2 + z_low, to_x)
                    at = (to_x * 2 + z_low) * ROWS
                    p[t, half, to_core, big, small] = value[at : at + ROWS]

    def part_copy(t, half):
        return send(p.at[t, half, 1 - core], rc.at[t, half], K_PART[t][half], partner)

    def part_add(t, half):
        part_copy(t, half).wait_recv()

        @pl.loop(0, 4)
        def _(b):
            p[t, half, core, b] = (
                p[t, half, core, b].astype(F32) + rc[t, half, b].astype(F32)
            ).astype(BF16)

    def big_sum_copy(t, half, o):
        return send(
            p.at[t, half, core, turn(big_pos[half], o)],
            big_in.at[t, half, o - 1],
            K_BIG[t][half][o],
            big_peers[half][o],
        )

    def small_sum_copy(t, half, o):
        return send(
            r1.at[t, half, turn(small_pos[half], o)],
            small_in.at[t, half, o - 1],
            K_SMALL[t][half][o],
            small_peers[half][o],
        )

    def decode_slot(t, log):
        for half in HALVES:
            decode(t, 1 - core, half)
            go(log, part_copy, t, half)
        for half in HALVES:
            decode(t, core, half)
            part_add(t, half)
            for o in (2, 1, 3):
                go(log, big_sum_copy, t, half, o)

    def big_sum(t, half, log):
        for o in OFFSETS:
            big_sum_copy(t, half, o).wait_recv()
        for i in range(4):
            value = p[t, half, core, big_pos[half], i].astype(F32)
            for o in OFFSETS:
                value = value + big_in[t, half, o - 1, i].astype(F32)
            r1[t, half, i] = value.astype(BF16)
        for o in (2, 1, 3):
            go(log, small_sum_copy, t, half, o)

    def small_sum(t, half):
        for o in OFFSETS:
            small_sum_copy(t, half, o).wait_recv()
        value = r1[t, half, small_pos[half]].astype(F32)
        for o in OFFSETS:
            value = value + small_in[t, half, o - 1].astype(F32)
        r2[t, half] = value.astype(BF16)

    def cross_send(half, from_y):
        return send(
            r2.at[1, half],
            cross_in.at[from_y],
            K_CROSS[from_y],
            place(x, 2 + half, z, core),
        )

    @pl.when(first_layer)
    def _():
        decode_slot(1, sent_first)

    decode_slot(0, sent)

    @pl.loop(0, 4)
    def _(n):
        cols = pl.ds(pl.multiple_of(n * 256, 256), 256)
        ft[cols, :] = feat[:, cols].T

    ft_store = pltpu.make_async_copy(ft, ft_out, local_sem.at[5])
    ft_store.start()

    for half in HALVES:

        @pl.loop(0, 4)
        def _(m):
            z_high, to_core = lax.div(m, 2), lax.rem(m, 2)
            block = column_block(g, (0,), half, z_high, to_core)
            rows = pl.ds(pl.multiple_of((half * 4 + m) * 256, 256), 256)
            gt[rows, :] = block.T

    gt_store = pltpu.make_async_copy(gt, gt_out, local_sem.at[6])
    gt_store.start()

    @pl.when(first_layer)
    def _():
        for half in HALVES:
            big_sum(1, half, sent_first)
        for half in HALVES:
            small_sum(1, half)
            for from_y in (0, 1):

                @pl.when(yb == from_y)
                def _():
                    cross_send(half, from_y).start()

    for half in HALVES:
        big_sum(0, half, sent)
    for half in HALVES:
        small_sum(0, half)
    y_copy = send(r2.at[0, 1 - yb], y_in, K_Y, y_pair)
    go(sent, lambda: y_copy)
    y_copy.wait_recv()
    total = r2[0, yb].astype(F32) + y_in[...].astype(F32) - tgt[...].astype(F32)
    rerr[...] = total

    @pl.when(second_layer)
    def _():
        for from_y in (0, 1):
            cross_send(0, from_y).wait_recv()
        rerr[...] = rerr[...] + cross_in[0].astype(F32) + cross_in[1].astype(F32)

    error = rerr[...]
    own_s = own_half(s, (LOSS_SCALE / TOK * error).astype(BF16))

    def back_copy(to_y, half):
        big, small = block_at(half, z, x)
        return send(
            own_s,
            s.at[1, half, core, big, small],
            K_BACK[half],
            place(x, to_y, z, core),
        )

    @pl.when(second_layer)
    def _():
        for half in HALVES:

            @pl.when(yb == half)
            def _():
                for to_y in (0, 1):
                    back_copy(to_y, half).start()

    s_y = send(own_s, own_s, K_GATHER[0]["y"], y_pair)
    go(sent, lambda: s_y)
    s0 = Gather(s, 0, K_GATHER[0], unlogged)
    s1 = Gather(s, 1, K_GATHER[1], sent_first)

    def s0_mine(mine, other):
        s0.small(mine)

    by_half(s0_mine)

    square = error * error
    tile = jnp.zeros((8, 128), F32)
    for i in range(8):
        for j in range(2):
            tile = tile + square[i * 8 : i * 8 + 8, j * 128 : j * 128 + 128]

    def square_copy(stage, o):
        peers = ([None, partner], x_peers, z_peers, y_peers)[stage]
        pos = (core, x, z, y)[stage]
        return send(
            squares_own.at[stage], squares_in.at[stage, pos], K_SQUARE[stage][o], peers[o]
        )

    def square_offsets(stage):
        return (1,) if stage == 0 else (1, 2, 3)

    def squares_start(stage, value):
        squares_own[stage] = value
        squares_in[stage, (core, x, z, y)[stage]] = value
        for o in square_offsets(stage):
            go(sent, square_copy, stage, o)

    def squares_end(stage):
        for o in square_offsets(stage):
            square_copy(stage, o).wait_recv()
        value = squares_in[stage, 0]
        for i in range(1, 2 if stage == 0 else 4):
            value = value + squares_in[stage, i]
        return value

    squares_start(0, tile)

    def feature_grad(t, n):
        rows = pl.ds(pl.multiple_of(n * 256, 256), 256)
        return lax.dot_general(
            all_columns(s, (t,)),
            decv[t, rows, :],
            (((1,), (1,)), ((), ())),
            preferred_element_type=F32,
        )

    def pg_copy(n):
        cols = pl.ds(pl.multiple_of(n * 256, 256), 256)
        return pltpu.make_async_copy(pg.at[:, cols], pg_out.at[:, cols], local_sem.at[7 + n])

    def preact_grad(n, value):
        cols = pl.ds(pl.multiple_of(n * 256, 256), 256)
        grad = jnp.where(pre[:, cols] > 0.0, value, 0.0).astype(BF16)
        pg[:, cols] = grad
        bg[:, cols] = jnp.sum(grad.astype(F32), 0, keepdims=True)
        pg_copy(n).start()

    def s0_other(mine, other):
        s_y.wait_recv()
        s0.small(other)

    by_half(s0_other)

    @pl.when(first_layer)
    def _():
        for half in HALVES:
            back_copy(0, half).wait_recv()
            s1.small(half)

    squares_start(1, squares_end(0))
    by_half(big_hops(s0))
    squares_start(2, squares_end(1))

    @pl.when(first_layer)
    def _():
        for half in HALVES:
            s1.big(half)

    squares_start(3, squares_end(2))
    by_half(share_hops(s0))
    msq[0, 0] = jnp.sum(squares_end(3)) / (LAYERS * TOK * D)
    s0.done()
    s_store0 = pltpu.make_async_copy(s.at[0], s_out.at[0], local_sem.at[2])
    s_store0.start()
    s_store1 = pltpu.make_async_copy(s.at[1], s_out.at[1], local_sem.at[3])

    @pl.when(second_layer)
    def _():
        @pl.loop(0, 4)
        def _(n):
            preact_grad(n, feature_grad(0, n))

    @pl.when(first_layer)
    def _():
        @pl.loop(0, 4)
        def _(n):
            rows = pl.ds(pl.multiple_of(n * 256, 256), 256)
            fg[:, rows] = feature_grad(0, n)

    @pl.when(first_layer)
    def _():
        for half in HALVES:
            s1.share(half)
        s1.done()
        s_store1.start()

    @pl.when(first_layer)
    def _():
        @pl.loop(0, 4)
        def _(n):
            rows = pl.ds(pl.multiple_of(n * 256, 256), 256)
            preact_grad(n, fg[:, rows] + feature_grad(1, n))

    drain(sent)
    for gather in (tokens, s0):
        for half in HALVES:
            for o in OFFSETS:
                gather.small_copy(half, o).wait_send()
                gather.big_copy(half, o).wait_send()
            for o in range(4):
                gather.shared_copy(half, o).wait_send()

    @pl.when(first_layer)
    def _():
        drain(sent_first)
        for half in HALVES:
            for from_y in (0, 1):

                @pl.when(yb == from_y)
                def _():
                    cross_send(half, from_y).wait_send()

        s_store1.wait()

    @pl.when(second_layer)
    def _():
        for half in HALVES:

            @pl.when(yb == half)
            def _():
                for to_y in (0, 1):
                    back_copy(to_y, half).wait_send()

    s_store0.wait()
    ft_store.wait()
    gt_store.wait()
    for n in range(4):
        pg_copy(n).wait()


def weight_grads_kernel(
    gt_in, ft_in, s_in, pg_in, rerr_in, msq_in, bg_in,
    dec_grad, enc_grad, rerr, msq, bg,
    gt, ft, s, pg, dec_out, enc_out, in_sem, dec_sem, enc_sem,
):
    y = lax.div(lax.axis_index("layer"), 4)
    first_layer = y < 2
    second_layer = y >= 2
    ft_copy = pltpu.make_async_copy(ft_in, ft, in_sem.at[0])
    s_copies = [pltpu.make_async_copy(s_in.at[t], s.at[t], in_sem.at[1 + t]) for t in (0, 1)]
    pg_copy = pltpu.make_async_copy(pg_in, pg, in_sem.at[3])
    gt_copy = pltpu.make_async_copy(gt_in, gt, in_sem.at[4])
    ft_copy.start()
    s_copies[0].start()

    @pl.when(first_layer)
    def _():
        s_copies[1].start()

    pg_copy.start()
    gt_copy.start()
    rerr[...] = rerr_in[...]
    bg[...] = bg_in[...]
    msq[0, 0] = msq_in[0, 0]

    def dec_copy(t, m):
        cols = pl.ds(pl.multiple_of(m * 256, 256), 256)
        return pltpu.make_async_copy(
            dec_out.at[t, m], dec_grad.at[t, :, cols], dec_sem.at[t, m]
        )

    def dec_half(t, half):
        @pl.loop(0, 4)
        def _(i):
            m = half * 4 + i
            block = column_block(s, (t,), half, lax.div(i, 2), lax.rem(i, 2))
            dec_out[t, m] = jnp.dot(
                ft[...], block, preferred_element_type=F32
            ).astype(BF16)
            dec_copy(t, m).start()

    @pl.when(second_layer)
    def _():
        @pl.loop(0, 8)
        def _(m):
            dec_out[1, m] = jnp.zeros((SHARD, 256), BF16)
            dec_copy(1, m).start()

    ft_copy.wait()
    s_copies[0].wait()
    dec_half(0, 0)
    dec_half(0, 1)

    @pl.when(first_layer)
    def _():
        s_copies[1].wait()
        dec_half(1, 0)
        dec_half(1, 1)

    pg_copy.wait()
    gt_copy.wait()

    def enc_copy(n):
        rows = pl.ds(pl.multiple_of(n * 512, 512), 512)
        return pltpu.make_async_copy(
            enc_out.at[rows, :], enc_grad.at[rows, :], enc_sem.at[n]
        )

    @pl.loop(0, 4)
    def _(n):
        rows = pl.ds(pl.multiple_of(n * 512, 512), 512)
        enc_out[rows, :] = jnp.dot(
            gt[rows, :], pg[...], preferred_element_type=F32
        ).astype(BF16)
        enc_copy(n).start()

    for t in (0, 1):
        for m in range(8):
            dec_copy(t, m).wait()
    for n in range(4):
        enc_copy(n).wait()


def on_device(tokens_in, targets, enc_weight, enc_bias, dec_weight):
    vmem = pl.BlockSpec(memory_space=pltpu.VMEM)
    smem = pl.BlockSpec(memory_space=pltpu.SMEM)
    anywhere = pl.BlockSpec(memory_space=pl.ANY)
    shape = jax.ShapeDtypeStruct
    blocks = (2, 2, 4, 4, ROWS, COLS)
    rerr, msq, gt, ft, s, pg, bg = pl.pallas_call(
        step_kernel,
        out_shape=(
            shape((ROWS, COLS), F32),
            shape((1, 1), F32),
            shape((D, TOK), BF16),
            shape((SHARD, TOK), BF16),
            shape((2, *blocks), BF16),
            shape((TOK, SHARD), BF16),
            shape((1, SHARD), F32),
        ),
        in_specs=[vmem, vmem, anywhere, vmem, anywhere],
        out_specs=(vmem, smem, anywhere, anywhere, anywhere, anywhere, vmem),
        scratch_shapes=[
            pltpu.VMEM((D, SHARD), BF16),
            pltpu.VMEM((2, SHARD, D), BF16),
            pltpu.VMEM((1, *blocks), BF16),
            pltpu.VMEM((TOK, SHARD), F32),
            pltpu.VMEM((TOK, SHARD), BF16),
            pltpu.VMEM((2, *blocks), BF16),
            pltpu.VMEM((2, 2, 4, 4, ROWS, COLS), BF16),
            pltpu.VMEM((2, 2, 3, 4, ROWS, COLS), BF16),
            pltpu.VMEM((2, 2, 4, ROWS, COLS), BF16),
            pltpu.VMEM((2, 2, 3, ROWS, COLS), BF16),
            pltpu.VMEM((2, 2, ROWS, COLS), BF16),
            pltpu.VMEM((ROWS, COLS), BF16),
            pltpu.VMEM((2, ROWS, COLS), BF16),
            pltpu.VMEM((2, *blocks), BF16),
            pltpu.VMEM((TOK, SHARD), F32),
            pltpu.VMEM((D, TOK), BF16),
            pltpu.VMEM((SHARD, TOK), BF16),
            pltpu.VMEM((TOK, SHARD), BF16),
            pltpu.VMEM((4, 4, 8, 128), F32),
            pltpu.VMEM((4, 8, 128), F32),
            pltpu.SemaphoreType.DMA((K_COUNT,)),
            pltpu.SemaphoreType.DMA((K_COUNT,)),
            pltpu.SemaphoreType.DMA((11,)),
        ],
        compiler_params=pltpu.CompilerParams(
            collective_id=0, has_side_effects=True, vmem_limit_bytes=60 * 2**20
        ),
        name="step",
    )(tokens_in, targets, enc_weight, enc_bias.reshape(1, SHARD), dec_weight)

    dec_grad, enc_grad, rerr, msq, bg = pl.pallas_call(
        weight_grads_kernel,
        out_shape=(
            shape((2, SHARD, D), BF16),
            shape((D, SHARD), BF16),
            shape((ROWS, COLS), F32),
            shape((1, 1), F32),
            shape((1, SHARD), F32),
        ),
        in_specs=[anywhere] * 4 + [vmem, smem, vmem],
        out_specs=(anywhere, anywhere, vmem, smem, vmem),
        scratch_shapes=[
            pltpu.VMEM((D, TOK), BF16),
            pltpu.VMEM((SHARD, TOK), BF16),
            pltpu.VMEM((2, *blocks), BF16),
            pltpu.VMEM((TOK, SHARD), BF16),
            pltpu.VMEM((2, 8, SHARD, 256), BF16),
            pltpu.VMEM((D, SHARD), BF16),
            pltpu.SemaphoreType.DMA((5,)),
            pltpu.SemaphoreType.DMA((2, 8)),
            pltpu.SemaphoreType.DMA((4,)),
        ],
        compiler_params=pltpu.CompilerParams(vmem_limit_bytes=60 * 2**20),
        name="weight_grads",
    )(gt, ft, s, pg, rerr, msq, bg)
    return (rerr, msq.reshape(()), enc_grad, bg.reshape(SHARD), dec_grad)


def solution(mesh):
    placed = (
        P("feat", "layer"),
        P("feat", "layer"),
        P(None, ("layer", "feat")),
        P(("layer", "feat")),
        P(None, ("layer", "feat"), None),
    )
    return jax.shard_map(
        on_device,
        mesh=mesh,
        in_specs=placed,
        out_specs=(
            P("feat", "layer"),
            P(),
            P(None, ("layer", "feat")),
            P(("layer", "feat")),
            P(None, ("layer", "feat"), None),
        ),
        check_vma=False,
    )
```

time: 726 us -> 99.3 us (0.14)
  waiting for transfers between devices: 557 us -> 0 us
  Pallas kernels: 0 us -> 98.4 us
  blocking collectives: 64.1 us -> 0 us
  matrix products: 35.4 us -> 0 us
  local copies, waits for them, and re-layouts: 24.7 us -> 0 us
  other arithmetic: 22 us -> 0 us
  between operations: 15.7 us -> 0.64 us
    all_gather x3 -> x0, waiting for transfers between devices: 366 us -> none  [the longest x1 238 us: on_device(): lax.all_gather(scaled[None], ('layer', 'feat'), axis=0, tiled=True)]
    psum x1 -> x0, waiting for transfers between devices: 185 us -> none  [on_device(): lax.psum(partial_value.astype(jnp.bfloat16), 'feat').astype(jnp.float32)]
    pallas_call x0 -> x2, Pallas kernels: none -> 98.4 us  [the longest x1 83.3 us: on_device(): pl.pallas_call(step_kernel, out_shape=(shape((ROWS, COLS), F32), shape((1...]
    psum x1 -> x0, blocking collectives: 64.1 us -> none  [on_device(): squares = lax.psum(jnp.sum(recon_error * recon_error), ('layer', 'feat'))]
    dot_general x5 -> x0, matrix products: 35.4 us -> none  [the longest x1 11.2 us: on_device(): jnp.einsum('tf,ktd->kfd', features, recon_grads, preferred_element_type=j...]
    unnamed x20 -> x0, local copies, waits for them, and re-layouts: 14.6 us -> none
    convert_element_type x3 -> x0, other arithmetic: 13.8 us -> none  [the longest x1 11.3 us: on_device(): gathered = lax.all_gather(summed_rows[None].astype(jnp.bfloat16), 'layer'...]
  transfers between devices with their start and end apart: 7 -> 0, of which waited for: 7 -> 0; matrix products, arithmetic and copies ran while one was open for 0% -> 0% of each run, Pallas kernels for 0% -> 0%
where the time goes in v2:
time: 99.3 us; the launch traced here: 99.1 us
  Pallas kernels  98.4 us (99%)
    pallas_call x1, Pallas kernels, on_device(): pl.pallas_call(step_kernel, out_shape=(shape((ROWS, COLS), F32), shape((1...  83.3 us
    pallas_call x1, Pallas kernels, on_device(): pl.pallas_call(weight_grads_kernel, out_shape=(shape((2, SHARD, D), BF16)...  15.1 us

profile of v2, /device:TPU:1, one launch (start us, length us, event | category | flops | bytes accessed | tf_op | source)
XLA Modules:
  0.0 99.1 jit_solution(9091594344868843935)
XLA Ops:
  0.6 83.3 %step.1 = (f32[64,256]{1,0:T(8,128)}, f32[1,1]{1,0:T(1,128)}, bf16[2048,512]{1,0:T(8,128)(2,1)}, bf16[1024,512]{1,0:T(8,128)(2,1)}, bf16[2,2,2,4,4,64,256]{6,5,4...) custom-call(bf16[64,256]{1,0:T(8,128)(2,1)} %tok.1, bf16[64,256]{1,0:T(8,128)(2,1)} %tgt.1, ...), custom_call_target="tpu_custom_call" | custom-call | tf_op jit(solution)/shard_map/step/pallas_call | solution.py:637
  84.0 15.1 %weight_grads.1 = (bf16[2,1024,2048]{2,1,0:T(8,128)(2,1)}, bf16[2048,1024]{1,0:T(8,128)(2,1)}, f32[64,256]{1,0:T(8,128)}, f32[1,1]{1,0:T(1,128)}, f32[1,1024]{1,0:T(1,128)}) custom-call(bf16[2048,512]{1,0:T(8,128)(2,1)} %get-tuple-element.17.gt_in, bf16[1024,512]{1,0:T(8,128)(2,1)} %get-tuple-element.18.ft_in, ...), custom_call_target="tpu_custom_call" | custom-call | tf_op jit(solution)/shard_map/weight_grads/pallas_call | solution.py:681

commit v3 on v2

v3 whole, which is shorter than its diff:
```python
import jax
import jax.numpy as jnp
from jax import lax
from jax.experimental import pallas as pl
from jax.experimental.pallas import tpu as pltpu
from jax.sharding import PartitionSpec as P

D = 2048
LAYERS = 2
TOK = 512
SHARD = 1024
ROWS = 64
COLS = 256
LOSS_SCALE = 64.0
MESH = pl.DeviceIdType.MESH
BF16 = jnp.bfloat16
F32 = jnp.float32


def place(x, y, z, core):
    return (y * 4 + lax.div(z, 2) * 2 + core, x * 2 + lax.rem(z, 2))


def block_at(half, z, x):
    return z * (1 - half) + x * half, x * (1 - half) + z * half


def column_block(ref, lead, half, z_high, core):
    pieces = []
    for x in range(4):
        for z_low in range(2):
            big, small = block_at(half, z_high * 2 + z_low, x)
            pieces.append(ref[(*lead, half, core, big, small)])
    return jnp.concatenate(pieces, 0)


def core_columns(ref, lead, core):
    return jnp.concatenate(
        [column_block(ref, lead, m // 2, m % 2, core) for m in range(4)], 1
    )


def core_shards(core):
    return [pl.ds(pl.multiple_of((m * 2 + core) * 256, 256), 256) for m in range(4)]


class Numbers:
    def __init__(self):
        self.count = 0

    def take(self, *dims):
        if not dims:
            self.count += 1
            return self.count - 1
        return [self.take(*dims[1:]) for _ in range(dims[0])]


NUMBERS = Numbers()
def gather_numbers():
    return dict(
        y=NUMBERS.take(),
        small=NUMBERS.take(2),
        big=NUMBERS.take(2, 4),
        shared=NUMBERS.take(),
    )


K_GATHER = [gather_numbers(), gather_numbers()]
K_PART = NUMBERS.take(2, 2)
K_BIG = NUMBERS.take(2, 2)
K_SMALL = NUMBERS.take(2, 2)
K_Y = NUMBERS.take()
K_CROSS = NUMBERS.take(2)
K_BACK = NUMBERS.take(2)
K_PASS = NUMBERS.take(2)
K_SQUARE = NUMBERS.take(4)
K_COUNT = NUMBERS.count


def step_kernel(
    tok, tgt_in, enc, bias_in, dec,
    rerr_out, squares_out, gt_out, ft_out, s_out, pg_out, bg_out,
    tgt, bias, rerr, bg, encv, decv, g, pre, feat, p, rc, big_in, r1, small_in, r2, y_in, cross_in,
    s, fg, gt, ft, pg, squares_in, squares_own, send_sem, recv_sem, local_sem,
):
    me_layer = lax.axis_index("layer")
    me_feat = lax.axis_index("feat")
    core = lax.rem(me_layer, 2)
    y = lax.div(me_layer, 4)
    x = lax.div(me_feat, 2)
    z = lax.rem(lax.div(me_layer, 2), 2) * 2 + lax.rem(me_feat, 2)
    yb = lax.rem(y, 2)
    first_layer = y < 2
    second_layer = y >= 2

    def turn(v, step):
        return lax.rem(v + step, 4)

    partner = place(x, y, z, 1 - core)
    y_pair = place(x, y + 1 - 2 * yb, z, core)
    x_peers = [None] + [place(turn(x, o), y, z, core) for o in (1, 2, 3)]
    y_peers = [None] + [place(x, turn(y, o), z, core) for o in (1, 2, 3)]
    z_peers = [None] + [place(x, y, turn(z, o), core) for o in (1, 2, 3)]
    big_pos, small_pos = (z, x), (x, z)
    big_peers, small_peers = (z_peers, x_peers), (x_peers, z_peers)
    HALVES = (0, 1)
    OFFSETS = (2, 1, 3)

    def send(src, dst, number, device):
        return pltpu.make_async_remote_copy(
            src_ref=src,
            dst_ref=dst,
            send_sem=send_sem.at[number],
            recv_sem=recv_sem.at[number],
            device_id=device,
            device_id_type=MESH,
        )

    def own_block(buf):
        big, small = block_at(yb, z, x)
        return buf.at[0, yb, core, big, small]

    enc_copy = pltpu.make_async_copy(enc, encv, local_sem.at[0])
    dec_copy = pltpu.make_async_copy(dec, decv, local_sem.at[1])
    tok_copy = pltpu.make_async_copy(tok, own_block(g), local_sem.at[2])
    tgt_copy = pltpu.make_async_copy(tgt_in, tgt, local_sem.at[3])
    bias_copy = pltpu.make_async_copy(bias_in, bias, local_sem.at[4])
    tok_copy.start()
    enc_copy.start()
    dec_copy.start()
    tgt_copy.start()
    bias_copy.start()

    barrier = pltpu.get_barrier_semaphore()
    for device in (partner, *x_peers[1:], *y_peers[1:], *z_peers[1:]):
        pl.semaphore_signal(barrier, inc=1, device_id=device, device_id_type=MESH)
    tok_copy.wait()
    pl.semaphore_wait(barrier, 10)

    class Gather:
        def __init__(self, buf, t, numbers, offsets=OFFSETS):
            self.buf, self.t, self.numbers = buf, t, numbers
            self.offsets = offsets

        def piece(self, half):
            return self.buf.at[self.t, half, core, big_pos[half], small_pos[half]]

        def chunk(self, half, i):
            return self.buf.at[self.t, half, core, i]

        def small_copy(self, half, o):
            ref = self.piece(half)
            return send(ref, ref, self.numbers["small"][half], small_peers[half][o])

        def all_small(self, half):
            ref = self.buf.at[self.t, half, core, 0, 0:3]
            return send(ref, ref, self.numbers["small"][half], partner)

        def big_copy(self, half, o):
            ref = self.chunk(half, big_pos[half])
            return send(ref, ref, self.numbers["big"][half][o], big_peers[half][o])

        def shared_copy(self, half, o):
            ref = self.chunk(half, turn(big_pos[half], 4 - o))
            return send(ref, ref, self.numbers["shared"], partner)

        def all_shared(self, of_core):
            ref = self.buf.at[self.t, :, of_core]
            return send(ref, ref, self.numbers["shared"], partner)

        def small(self, half):
            for o in OFFSETS:
                self.small_copy(half, o).start()

        def big(self, half):
            self.all_small(half).wait_recv()
            for o in self.offsets:
                self.big_copy(half, o).start()
            self.shared_copy(half, 0).start()

        def share(self, half):
            for o in self.offsets:
                self.big_copy(half, o).wait_recv()
                self.shared_copy(half, o).start()

        def done(self):
            self.all_shared(1 - core).wait_recv()

        def drain(self):
            for half in HALVES:
                self.all_small(half).wait_send()
                for o in self.offsets:
                    self.big_copy(half, o).wait_send()
            self.all_shared(core).wait_send()

    def by_half(fn):
        @pl.when(yb == 0)
        def _():
            fn(0, 1)

        @pl.when(yb == 1)
        def _():
            fn(1, 0)

    own = own_block(g)
    tok_y = send(own, own, K_GATHER[0]["y"], y_pair)
    tok_y.start()
    def first_hops(gather, y_copy):
        def run(mine, other):
            gather.small(mine)
            y_copy.wait_recv()
            gather.small(other)

        return run

    tokens = Gather(g, 0, K_GATHER[0])
    by_half(first_hops(tokens, tok_y))

    def big_hops(gather):
        def run(mine, other):
            gather.big(mine)
            gather.big(other)

        return run

    by_half(big_hops(tokens))

    def share_hops(gather):
        def run(mine, other):
            gather.share(mine)
            gather.share(other)

        return run

    by_half(share_hops(tokens))
    enc_copy.wait()
    bias_copy.wait()

    def encode_part(from_core, n):
        cols = pl.ds(pl.multiple_of(n * 256, 256), 256)
        weights = jnp.concatenate([encv[rows, cols] for rows in core_shards(from_core)], 0)
        return cols, jnp.dot(
            core_columns(g, (0,), from_core), weights, preferred_element_type=F32
        )

    @pl.loop(0, 4)
    def _(n):
        cols, value = encode_part(core, n)
        pre[:, cols] = value + bias[:, cols]

    tokens.done()

    @pl.loop(0, 4)
    def _(n):
        cols, value = encode_part(1 - core, n)
        act = pre[:, cols] + value
        pre[:, cols] = act
        feat[:, cols] = jnp.maximum(act, 0.0).astype(BF16)

    dec_copy.wait()

    def decode(t, to_core, half):
        for z_high in range(2):
            first = pl.multiple_of((half * 4 + z_high * 2 + to_core) * 256, 256)
            value = jnp.dot(
                feat[...], decv[t, :, pl.ds(first, 256)], preferred_element_type=F32
            ).astype(BF16)
            for to_x in range(4):
                for z_low in range(2):
                    big, small = block_at(half, z_high * 2 + z_low, to_x)
                    at = (to_x * 2 + z_low) * ROWS
                    p[t, half, to_core, big, small] = value[at : at + ROWS]

    def part_copy(t, half):
        return send(p.at[t, half, 1 - core], rc.at[t, half], K_PART[t][half], partner)

    def part_add(t, half):
        part_copy(t, half).wait_recv()

        @pl.loop(0, 4)
        def _(b):
            p[t, half, core, b] = (
                p[t, half, core, b].astype(F32) + rc[t, half, b].astype(F32)
            ).astype(BF16)

    def big_sum_copy(t, half, o):
        return send(
            p.at[t, half, core, turn(big_pos[half], o)],
            big_in.at[t, half, o - 1],
            K_BIG[t][half],
            big_peers[half][o],
        )

    def all_big_sums(t, half):
        return send(p.at[t, half, core, 0:3], big_in.at[t, half], K_BIG[t][half], partner)

    def small_sum_copy(t, half, o):
        return send(
            r1.at[t, half, turn(small_pos[half], o)],
            small_in.at[t, half, o - 1],
            K_SMALL[t][half],
            small_peers[half][o],
        )

    def all_small_sums(t, half):
        return send(r1.at[t, half, 0:3], small_in.at[t, half], K_SMALL[t][half], partner)

    def big_sum_send(t, half):
        for o in OFFSETS:
            big_sum_copy(t, half, o).start()

    def decode_slot(t, after):
        for half in HALVES:
            decode(t, 1 - core, half)
            part_copy(t, half).start()
        for half in HALVES:
            decode(t, core, half)
            part_add(t, half)
            after(half)

    def big_sum(t, half):
        all_big_sums(t, half).wait_recv()
        for i in range(4):
            value = p[t, half, core, big_pos[half], i].astype(F32)
            for o in OFFSETS:
                value = value + big_in[t, half, o - 1, i].astype(F32)
            r1[t, half, i] = value.astype(BF16)
        for o in OFFSETS:
            small_sum_copy(t, half, o).start()

    def small_sum(t, half):
        all_small_sums(t, half).wait_recv()
        value = r1[t, half, small_pos[half]].astype(F32)
        for o in OFFSETS:
            value = value + small_in[t, half, o - 1].astype(F32)
        r2[t, half] = value.astype(BF16)

    def cross_send(half, from_y):
        return send(
            r2.at[1, half],
            cross_in.at[from_y],
            K_CROSS[from_y],
            place(x, 2 + half, z, core),
        )

    @pl.when(first_layer)
    def _():
        decode_slot(1, lambda half: big_sum_send(1, half))

    def send_early(half):
        @pl.when(second_layer)
        def _():
            big_sum_send(0, half)

    decode_slot(0, send_early)

    @pl.loop(0, 4)
    def _(n):
        cols = pl.ds(pl.multiple_of(n * 256, 256), 256)
        ft[cols, :] = feat[:, cols].T

    ft_store = pltpu.make_async_copy(ft, ft_out, local_sem.at[0])
    ft_store.start()

    for half in HALVES:

        @pl.loop(0, 4)
        def _(m):
            z_high, to_core = lax.div(m, 2), lax.rem(m, 2)
            block = column_block(g, (0,), half, z_high, to_core)
            rows = pl.ds(pl.multiple_of((half * 4 + m) * 256, 256), 256)
            gt[rows, :] = block.T

    gt_store = pltpu.make_async_copy(gt, gt_out, local_sem.at[1])
    gt_store.start()

    @pl.when(first_layer)
    def _():
        for half in HALVES:
            big_sum(1, half)
        for half in HALVES:
            big_sum_send(0, half)
        for half in HALVES:
            small_sum(1, half)
            for from_y in (0, 1):

                @pl.when(yb == from_y)
                def _():
                    cross_send(half, from_y).start()

    for half in HALVES:
        big_sum(0, half)

    tok_y.wait_send()
    tokens.drain()
    s0 = Gather(s, 0, K_GATHER[0])
    s1 = Gather(s, 1, K_GATHER[1], (1, 3))

    def back_copy(to_y, half):
        big, small = block_at(half, z, x)
        return send(
            own_block(s),
            s.at[1, half, core, big, small],
            K_BACK[half],
            place(x, to_y, z, core),
        )

    def pass_copy(half):
        opposite = turn(big_pos[half], 2)
        return send(
            s.at[0, half, core, opposite],
            s.at[1, half, core, opposite],
            K_PASS[half],
            place(x, 3 - y, z, core),
        )

    @pl.when(first_layer)
    def _():
        for half in HALVES:
            back_copy(0, half).wait_recv()
            s1.small(half)

    for half in HALVES:
        small_sum(0, half)
    y_copy = send(r2.at[0, 1 - yb], y_in, K_Y, y_pair)
    y_copy.start()

    @pl.when(first_layer)
    def _():
        for half in HALVES:
            s1.big(half)

    y_copy.wait_recv()
    tgt_copy.wait()
    total = r2[0, yb].astype(F32) + y_in[...].astype(F32) - tgt[...].astype(F32)
    rerr[...] = total

    @pl.when(second_layer)
    def _():
        for from_y in (0, 1):
            cross_send(0, from_y).wait_recv()
        rerr[...] = rerr[...] + cross_in[0].astype(F32) + cross_in[1].astype(F32)

    error = rerr[...]
    own_s = own_block(s)
    own_s[...] = (LOSS_SCALE / TOK * error).astype(BF16)

    @pl.when(second_layer)
    def _():
        for half in HALVES:

            @pl.when(yb == half)
            def _():
                for to_y in (0, 1):
                    back_copy(to_y, half).start()

    s_y = send(own_s, own_s, K_GATHER[0]["y"], y_pair)
    s_y.start()

    def s0_mine(mine, other):
        s0.small(mine)

    by_half(s0_mine)
    rerr_copy = pltpu.make_async_copy(rerr, rerr_out, local_sem.at[11])
    rerr_copy.start()

    square = error * error
    tile = jnp.zeros((8, 128), F32)
    for i in range(8):
        for j in range(2):
            tile = tile + square[i * 8 : i * 8 + 8, j * 128 : j * 128 + 128]

    def square_copy(stage, o):
        peers = (x_peers, z_peers, y_peers, [None, partner])[stage]
        pos = (x, z, y, core)[stage]
        return send(
            squares_own.at[stage], squares_in.at[stage, pos], K_SQUARE[stage], peers[o]
        )

    def square_offsets(stage):
        return (1, 2, 3) if stage < 3 else (1,)

    def all_squares(stage):
        ref = squares_in.at[stage, 0 : len(square_offsets(stage))]
        return send(ref, ref, K_SQUARE[stage], partner)

    def squares_start(stage, value):
        squares_own[stage] = value
        squares_in[stage, (x, z, y, core)[stage]] = value
        for o in square_offsets(stage):
            square_copy(stage, o).start()

    def squares_end(stage):
        all_squares(stage).wait_recv()
        value = squares_in[stage, 0]
        for i in range(1, 4 if stage < 3 else 2):
            value = value + squares_in[stage, i]
        return value

    squares_start(0, tile)

    def feature_grad(t, from_core, n):
        rows = pl.ds(pl.multiple_of(n * 256, 256), 256)
        weights = jnp.concatenate(
            [decv[t, rows, cols] for cols in core_shards(from_core)], 1
        )
        return rows, lax.dot_general(
            core_columns(s, (t,), from_core),
            weights,
            (((1,), (1,)), ((), ())),
            preferred_element_type=F32,
        )

    def pg_copy(n):
        cols = pl.ds(pl.multiple_of(n * 256, 256), 256)
        return pltpu.make_async_copy(pg.at[:, cols], pg_out.at[:, cols], local_sem.at[7 + n])

    def grad_start(t, from_core):
        @pl.loop(0, 4)
        def _(n):
            cols, value = feature_grad(t, from_core, n)
            fg[:, cols] = value

    def grad_more(t, from_core):
        @pl.loop(0, 4)
        def _(n):
            cols, value = feature_grad(t, from_core, n)
            fg[:, cols] = fg[:, cols] + value

    def grad_end(t, from_core):
        @pl.loop(0, 4)
        def _(n):
            cols, value = feature_grad(t, from_core, n)
            grad = jnp.where(pre[:, cols] > 0.0, fg[:, cols] + value, 0.0).astype(BF16)
            pg[:, cols] = grad
            bg[:, cols] = jnp.sum(grad.astype(F32), 0, keepdims=True)
            pg_copy(n).start()

    def s0_other(mine, other):
        s_y.wait_recv()
        s0.small(other)

    by_half(s0_other)
    squares_start(1, squares_end(0))
    by_half(big_hops(s0))

    s_store0 = pltpu.make_async_copy(s.at[0], s_out.at[0], local_sem.at[5])
    s_store1 = pltpu.make_async_copy(s.at[1], s_out.at[1], local_sem.at[6])

    @pl.when(second_layer)
    def _():
        for half in HALVES:
            s0.big_copy(half, 2).wait_recv()
            pass_copy(half).start()
            s0.shared_copy(half, 2).start()
        for half in HALVES:
            for o in (1, 3):
                s0.big_copy(half, o).wait_recv()
                s0.shared_copy(half, o).start()

    @pl.when(first_layer)
    def _():
        for half in HALVES:
            s1.share(half)

    squares_start(2, squares_end(1))

    @pl.when(first_layer)
    def _():
        for half in HALVES:
            pass_copy(half).wait_recv()
            s1.shared_copy(half, 2).start()

    squares_start(3, squares_end(2))

    @pl.when(first_layer)
    def _():
        grad_start(1, core)

    @pl.when(first_layer)
    def _():
        for half in HALVES:
            s0.share(half)
        s1.done()
        s_store1.start()

    @pl.when(first_layer)
    def _():
        grad_more(1, 1 - core)
        grad_more(0, core)

    @pl.when(second_layer)
    def _():
        grad_start(0, core)

    squares_own[4] = squares_end(3)
    squares_copy = pltpu.make_async_copy(squares_own.at[4], squares_out, local_sem.at[12])
    squares_copy.start()

    s0.done()
    s_store0.start()
    grad_end(0, 1 - core)
    bg_copy = pltpu.make_async_copy(bg, bg_out, local_sem.at[13])
    bg_copy.start()

    def drain_sums(t):
        for half in HALVES:
            part_copy(t, half).wait_send()
            all_big_sums(t, half).wait_send()
            all_small_sums(t, half).wait_send()

    drain_sums(0)
    y_copy.wait_send()
    s_y.wait_send()
    s0.drain()
    for stage in range(4):
        all_squares(stage).wait_send()

    @pl.when(first_layer)
    def _():
        drain_sums(1)
        s1.drain()
        for half in HALVES:
            for from_y in (0, 1):

                @pl.when(yb == from_y)
                def _():
                    cross_send(half, from_y).wait_send()

        s_store1.wait()

    @pl.when(second_layer)
    def _():
        for half in HALVES:

            @pl.when(yb == half)
            def _():
                for to_y in (0, 1):
                    back_copy(to_y, half).wait_send()

            pass_copy(half).wait_send()

    s_store0.wait()
    rerr_copy.wait()
    squares_copy.wait()
    bg_copy.wait()
    ft_store.wait()
    gt_store.wait()
    for n in range(4):
        pg_copy(n).wait()


def weight_grads_kernel(
    gt_in, ft_in, s_in, pg_in, rerr_in, squares_in, bg_in,
    dec_grad, enc_grad, rerr_out, mean_out, bg_out,
    gt, ft, s, pg, rerr, squares, mean, bg, dec_out, enc_out,
    in_sem, dec_sem, enc_sem, small_sem,
):
    y = lax.div(lax.axis_index("layer"), 4)
    first_layer = y < 2
    second_layer = y >= 2
    ft_copy = pltpu.make_async_copy(ft_in, ft, in_sem.at[0])
    s_copies = [
        [
            pltpu.make_async_copy(s_in.at[t, half], s.at[t, half], in_sem.at[1 + 2 * t + half])
            for half in (0, 1)
        ]
        for t in (0, 1)
    ]
    pg_copy = pltpu.make_async_copy(pg_in, pg, in_sem.at[5])
    gt_copy = pltpu.make_async_copy(gt_in, gt, in_sem.at[6])
    ft_copy.start()
    for copy in s_copies[0]:
        copy.start()

    @pl.when(first_layer)
    def _():
        for copy in s_copies[1]:
            copy.start()

    pg_copy.start()
    gt_copy.start()
    small_in = [
        pltpu.make_async_copy(src, dst, small_sem.at[i])
        for i, (src, dst) in enumerate(((rerr_in, rerr), (squares_in, squares), (bg_in, bg)))
    ]
    small_out = [
        pltpu.make_async_copy(src, dst, small_sem.at[3 + i])
        for i, (src, dst) in enumerate(((rerr, rerr_out), (mean, mean_out), (bg, bg_out)))
    ]
    for copy in small_in:
        copy.start()

    def dec_copy(t, m):
        cols = pl.ds(pl.multiple_of(m * 256, 256), 256)
        return pltpu.make_async_copy(
            dec_out.at[t, m], dec_grad.at[t, :, cols], dec_sem.at[t, m]
        )

    def dec_half(t, half):
        s_copies[t][half].wait()

        @pl.loop(0, 4, unroll=2)
        def _(i):
            m = half * 4 + i
            block = column_block(s, (t,), half, lax.div(i, 2), lax.rem(i, 2))
            dec_out[t, m] = jnp.dot(
                ft[...], block, preferred_element_type=F32
            ).astype(BF16)
            dec_copy(t, m).start()

    @pl.when(second_layer)
    def _():
        @pl.loop(0, 8)
        def _(m):
            dec_out[1, m] = jnp.zeros((SHARD, 256), BF16)
            dec_copy(1, m).start()

    ft_copy.wait()
    dec_half(0, 0)
    dec_half(0, 1)

    @pl.when(first_layer)
    def _():
        dec_half(1, 0)
        dec_half(1, 1)

    for copy in small_in:
        copy.wait()
    mean[...] = jnp.sum(squares[...], keepdims=True) / (LAYERS * TOK * D)
    for copy in small_out:
        copy.start()
    pg_copy.wait()
    gt_copy.wait()

    def enc_copy(n):
        rows = pl.ds(pl.multiple_of(n * 512, 512), 512)
        return pltpu.make_async_copy(
            enc_out.at[rows, :], enc_grad.at[rows, :], enc_sem.at[n]
        )

    @pl.loop(0, 4)
    def _(n):
        rows = pl.ds(pl.multiple_of(n * 512, 512), 512)
        enc_out[rows, :] = jnp.dot(
            gt[rows, :], pg[...], preferred_element_type=F32
        ).astype(BF16)
        enc_copy(n).start()

    for t in (0, 1):
        for m in range(8):
            dec_copy(t, m).wait()
    for n in range(4):
        enc_copy(n).wait()
    for copy in small_out:
        copy.wait()


def on_device(tokens_in, targets, enc_weight, enc_bias, dec_weight):
    anywhere = pl.BlockSpec(memory_space=pl.ANY)
    shape = jax.ShapeDtypeStruct
    blocks = (2, 2, 4, 4, ROWS, COLS)
    rerr, squares, gt, ft, s, pg, bg = pl.pallas_call(
        step_kernel,
        out_shape=(
            shape((ROWS, COLS), F32),
            shape((8, 128), F32),
            shape((D, TOK), BF16),
            shape((SHARD, TOK), BF16),
            shape((2, *blocks), BF16),
            shape((TOK, SHARD), BF16),
            shape((1, SHARD), F32),
        ),
        in_specs=[anywhere] * 5,
        out_specs=[anywhere] * 7,
        scratch_shapes=[
            pltpu.VMEM((ROWS, COLS), BF16),
            pltpu.VMEM((1, SHARD), F32),
            pltpu.VMEM((ROWS, COLS), F32),
            pltpu.VMEM((1, SHARD), F32),
            pltpu.VMEM((D, SHARD), BF16),
            pltpu.VMEM((2, SHARD, D), BF16),
            pltpu.VMEM((1, *blocks), BF16),
            pltpu.VMEM((TOK, SHARD), F32),
            pltpu.VMEM((TOK, SHARD), BF16),
            pltpu.VMEM((2, *blocks), BF16),
            pltpu.VMEM((2, 2, 4, 4, ROWS, COLS), BF16),
            pltpu.VMEM((2, 2, 3, 4, ROWS, COLS), BF16),
            pltpu.VMEM((2, 2, 4, ROWS, COLS), BF16),
            pltpu.VMEM((2, 2, 3, ROWS, COLS), BF16),
            pltpu.VMEM((2, 2, ROWS, COLS), BF16),
            pltpu.VMEM((ROWS, COLS), BF16),
            pltpu.VMEM((2, ROWS, COLS), BF16),
            pltpu.VMEM((2, *blocks), BF16),
            pltpu.VMEM((TOK, SHARD), F32),
            pltpu.VMEM((D, TOK), BF16),
            pltpu.VMEM((SHARD, TOK), BF16),
            pltpu.VMEM((TOK, SHARD), BF16),
            pltpu.VMEM((4, 4, 8, 128), F32),
            pltpu.VMEM((5, 8, 128), F32),
            pltpu.SemaphoreType.DMA((K_COUNT,)),
            pltpu.SemaphoreType.DMA((K_COUNT,)),
            pltpu.SemaphoreType.DMA((14,)),
        ],
        compiler_params=pltpu.CompilerParams(
            collective_id=0, has_side_effects=True, vmem_limit_bytes=60 * 2**20
        ),
        name="step",
    )(tokens_in, targets, enc_weight, enc_bias.reshape(1, SHARD), dec_weight)

    dec_grad, enc_grad, rerr, mean, bg = pl.pallas_call(
        weight_grads_kernel,
        out_shape=(
            shape((2, SHARD, D), BF16),
            shape((D, SHARD), BF16),
            shape((ROWS, COLS), F32),
            shape((1, 1), F32),
            shape((1, SHARD), F32),
        ),
        in_specs=[anywhere] * 7,
        out_specs=[anywhere] * 5,
        scratch_shapes=[
            pltpu.VMEM((D, TOK), BF16),
            pltpu.VMEM((SHARD, TOK), BF16),
            pltpu.VMEM((2, *blocks), BF16),
            pltpu.VMEM((TOK, SHARD), BF16),
            pltpu.VMEM((ROWS, COLS), F32),
            pltpu.VMEM((8, 128), F32),
            pltpu.VMEM((1, 1), F32),
            pltpu.VMEM((1, SHARD), F32),
            pltpu.VMEM((2, 8, SHARD, 256), BF16),
            pltpu.VMEM((D, SHARD), BF16),
            pltpu.SemaphoreType.DMA((7,)),
            pltpu.SemaphoreType.DMA((2, 8)),
            pltpu.SemaphoreType.DMA((4,)),
            pltpu.SemaphoreType.DMA((6,)),
        ],
        compiler_params=pltpu.CompilerParams(vmem_limit_bytes=60 * 2**20),
        name="weight_grads",
    )(gt, ft, s, pg, rerr, squares, bg)
    return (rerr, mean.reshape(()), enc_grad, bg.reshape(SHARD), dec_grad)


def solution(mesh):
    placed = (
        P("feat", "layer"),
        P("feat", "layer"),
        P(None, ("layer", "feat")),
        P(("layer", "feat")),
        P(None, ("layer", "feat"), None),
    )
    return jax.shard_map(
        on_device,
        mesh=mesh,
        in_specs=placed,
        out_specs=(
            P("feat", "layer"),
            P(),
            P(None, ("layer", "feat")),
            P(("layer", "feat")),
            P(None, ("layer", "feat"), None),
        ),
        check_vma=False,
    )
```

time: 99.3 us -> 88.9 us (0.90)
  Pallas kernels: 98.4 us -> 87.4 us
    pallas_call x1, Pallas kernels: 83.3 us -> 75.5 us  [on_device(): pl.pallas_call(step_kernel, out_shape=(shape((ROWS, COLS), F32), shape((8...]
    pallas_call x1, Pallas kernels: 15.1 us -> 11.9 us  [on_device(): pl.pallas_call(weight_grads_kernel, out_shape=(shape((2, SHARD, D), BF16)...]
where the time goes in v3:
time: 88.9 us; the launch traced here: 88 us
  Pallas kernels  87.4 us (98%)
    pallas_call x1, Pallas kernels, on_device(): pl.pallas_call(step_kernel, out_shape=(shape((ROWS, COLS), F32), shape((8...  75.5 us
    pallas_call x1, Pallas kernels, on_device(): pl.pallas_call(weight_grads_kernel, out_shape=(shape((2, SHARD, D), BF16)...  11.9 us

profile of v3, /device:TPU:1, one launch (start us, length us, event | category | flops | bytes accessed | tf_op | source)
XLA Modules:
  0.0 88.0 jit_solution(8203916310741632184)
XLA Ops:
  0.6 75.5 %step.1 = (f32[64,256]{1,0:T(8,128)}, f32[8,128]{1,0:T(8,128)}, bf16[2048,512]{1,0:T(8,128)(2,1)}, bf16[1024,512]{1,0:T(8,128)(2,1)}, bf16[2,2,2,4,4,64,256]{6,5...) custom-call(bf16[64,256]{1,0:T(8,128)(2,1)} %tok.1, bf16[64,256]{1,0:T(8,128)(2,1)} %tgt_in.1, ...), custom_call_target="tpu_custom_call" | custom-call | tf_op jit(solution)/shard_map/step/pallas_call | solution.py:763
  76.2 11.9 %weight_grads.1 = (bf16[2,1024,2048]{2,1,0:T(8,128)(2,1)}, bf16[2048,1024]{1,0:T(8,128)(2,1)}, f32[64,256]{1,0:T(8,128)}, f32[1,1]{1,0:T(1,128)}, f32[1,1024]{1,0:T(1,128)}) custom-call(bf16[2048,512]{1,0:T(8,128)(2,1)} %get-tuple-element.17.gt_in, bf16[1024,512]{1,0:T(8,128)(2,1)} %get-tuple-element.18.ft_in, ...), custom_call_target="tpu_custom_call" | custom-call | tf_op jit(solution)/shard_map/weight_grads/pallas_call | solution.py:811

commit v4 on v3

--- a/solution.py
+++ b/solution.py
@@ -13,6 +13,9 @@
 COLS = 256
 LOSS_SCALE = 64.0
 MESH = pl.DeviceIdType.MESH
+HELD = (2,)
+PASS = (0, 1)
+ORDER = (0, 1)
 BF16 = jnp.bfloat16
 F32 = jnp.float32
 
@@ -40,6 +43,12 @@
     )
 
 
+def all_columns(ref, lead):
+    return jnp.concatenate(
+        [column_block(ref, lead, m // 4, m // 2 % 2, m % 2) for m in range(8)], 1
+    )
+
+
 def core_shards(core):
     return [pl.ds(pl.multiple_of((m * 2 + core) * 256, 256), 256) for m in range(4)]
 
@@ -58,7 +67,6 @@
 NUMBERS = Numbers()
 def gather_numbers():
     return dict(
-        y=NUMBERS.take(),
         small=NUMBERS.take(2),
         big=NUMBERS.take(2, 4),
         shared=NUMBERS.take(),
@@ -68,8 +76,8 @@
 K_GATHER = [gather_numbers(), gather_numbers()]
 K_PART = NUMBERS.take(2, 2)
 K_BIG = NUMBERS.take(2, 2)
-K_SMALL = NUMBERS.take(2, 2)
-K_Y = NUMBERS.take()
+K_SMALL = NUMBERS.take(2)
+K_FINAL = NUMBERS.take()
 K_CROSS = NUMBERS.take(2)
 K_BACK = NUMBERS.take(2)
 K_PASS = NUMBERS.take(2)
@@ -80,7 +88,7 @@
 def step_kernel(
     tok, tgt_in, enc, bias_in, dec,
     rerr_out, squares_out, gt_out, ft_out, s_out, pg_out, bg_out,
-    tgt, bias, rerr, bg, encv, decv, g, pre, feat, p, rc, big_in, r1, small_in, r2, y_in, cross_in,
+    tgt, bias, rerr, bg, encv, decv, g, pre, feat, p, rc, big_in, r1, small_in, r2, final_in, cross_in,
     s, fg, gt, ft, pg, squares_in, squares_own, send_sem, recv_sem, local_sem,
 ):
     me_layer = lax.axis_index("layer")
@@ -97,12 +105,16 @@
         return lax.rem(v + step, 4)
 
     partner = place(x, y, z, 1 - core)
-    y_pair = place(x, y + 1 - 2 * yb, z, core)
+    y_pair = y + 1 - 2 * yb
     x_peers = [None] + [place(turn(x, o), y, z, core) for o in (1, 2, 3)]
     y_peers = [None] + [place(x, turn(y, o), z, core) for o in (1, 2, 3)]
     z_peers = [None] + [place(x, y, turn(z, o), core) for o in (1, 2, 3)]
     big_pos, small_pos = (z, x), (x, z)
     big_peers, small_peers = (z_peers, x_peers), (x_peers, z_peers)
+    pair_peers = (
+        [place(turn(x, o), y_pair, z, core) for o in range(4)],
+        [place(x, y_pair, turn(z, o), core) for o in range(4)],
+    )
     HALVES = (0, 1)
     OFFSETS = (2, 1, 3)
 
@@ -132,13 +144,20 @@
     bias_copy.start()
 
     barrier = pltpu.get_barrier_semaphore()
-    for device in (partner, *x_peers[1:], *y_peers[1:], *z_peers[1:]):
+    for device in (
+        partner,
+        *x_peers[1:],
+        *y_peers[1:],
+        *z_peers[1:],
+        *pair_peers[0][1:],
+        *pair_peers[1][1:],
+    ):
         pl.semaphore_signal(barrier, inc=1, device_id=device, device_id_type=MESH)
     tok_copy.wait()
-    pl.semaphore_wait(barrier, 10)
+    pl.semaphore_wait(barrier, 16)
 
     class Gather:
-        def __init__(self, buf, t, numbers, offsets=OFFSETS):
+        def __init__(self, buf, t, numbers, offsets=(OFFSETS, OFFSETS)):
             self.buf, self.t, self.numbers = buf, t, numbers
             self.offsets = offsets
 
@@ -152,9 +171,22 @@
             ref = self.piece(half)
             return send(ref, ref, self.numbers["small"][half], small_peers[half][o])
 
-        def all_small(self, half):
-            ref = self.buf.at[self.t, half, core, 0, 0:3]
+        def pair_copy(self, half, o):
+            ref = self.piece(half)
+            return send(ref, ref, self.numbers["small"][half], pair_peers[half][o])
+
+        def all_small(self, half, count=3):
+            ref = self.buf.at[self.t, half, core, 0, 0:count]
             return send(ref, ref, self.numbers["small"][half], partner)
+
+        def all_joint(self, half):
+            return send(final_in, final_in, self.numbers["small"][half], partner)
+
+        def joint(self, mine, other):
+            for o in (2, 1, 3, 0):
+                self.pair_copy(mine, o).start()
+                if o > 0:
+                    self.small_copy(mine, o).start()
 
         def big_copy(self, half, o):
             ref = self.chunk(half, big_pos[half])
@@ -172,24 +204,27 @@
             for o in OFFSETS:
                 self.small_copy(half, o).start()
 
-        def big(self, half):
-            self.all_small(half).wait_recv()
-            for o in self.offsets:
+        def big(self, half, count=3):
+            self.all_small(half, count).wait_recv()
+            for o in self.offsets[half]:
                 self.big_copy(half, o).start()
             self.shared_copy(half, 0).start()
 
         def share(self, half):
-            for o in self.offsets:
+            for o in self.offsets[half]:
                 self.big_copy(half, o).wait_recv()
                 self.shared_copy(half, o).start()
 
         def done(self):
             self.all_shared(1 - core).wait_recv()
 
-        def drain(self):
+        def drain(self, joint):
+            if joint:
+                by_half(lambda mine, other: self.all_joint(mine).wait_send())
             for half in HALVES:
-                self.all_small(half).wait_send()
-                for o in self.offsets:
+                if not joint:
+                    self.all_small(half).wait_send()
+                for o in self.offsets[half]:
                     self.big_copy(half, o).wait_send()
             self.all_shared(core).wait_send()
 
@@ -202,24 +237,13 @@
         def _():
             fn(1, 0)
 
-    own = own_block(g)
-    tok_y = send(own, own, K_GATHER[0]["y"], y_pair)
-    tok_y.start()
-    def first_hops(gather, y_copy):
-        def run(mine, other):
-            gather.small(mine)
-            y_copy.wait_recv()
-            gather.small(other)
-
-        return run
-
     tokens = Gather(g, 0, K_GATHER[0])
-    by_half(first_hops(tokens, tok_y))
+    by_half(tokens.joint)
 
     def big_hops(gather):
         def run(mine, other):
             gather.big(mine)
-            gather.big(other)
+            gather.big(other, 4)
 
         return run
 
@@ -243,14 +267,14 @@
             core_columns(g, (0,), from_core), weights, preferred_element_type=F32
         )
 
-    @pl.loop(0, 4)
+    @pl.loop(0, 4, unroll=2)
     def _(n):
         cols, value = encode_part(core, n)
         pre[:, cols] = value + bias[:, cols]
 
     tokens.done()
 
-    @pl.loop(0, 4)
+    @pl.loop(0, 4, unroll=2)
     def _(n):
         cols, value = encode_part(1 - core, n)
         act = pre[:, cols] + value
@@ -294,19 +318,37 @@
     def all_big_sums(t, half):
         return send(p.at[t, half, core, 0:3], big_in.at[t, half], K_BIG[t][half], partner)
 
-    def small_sum_copy(t, half, o):
+    def small_sum_copy(half, o):
         return send(
-            r1.at[t, half, turn(small_pos[half], o)],
-            small_in.at[t, half, o - 1],
-            K_SMALL[t][half],
+            r1.at[1, half, turn(small_pos[half], o)],
+            small_in.at[half, o - 1],
+            K_SMALL[half],
             small_peers[half][o],
         )
 
-    def all_small_sums(t, half):
-        return send(r1.at[t, half, 0:3], small_in.at[t, half], K_SMALL[t][half], partner)
-
-    def big_sum_send(t, half):
+    def all_small_sums(half):
+        return send(r1.at[1, half, 0:3], small_in.at[half], K_SMALL[half], partner)
+
+    def final_copy(half, o, pair):
+        return send(
+            r1.at[0, half, turn(small_pos[half], o)],
+            final_in.at[3 + o if pair else o - 1],
+            K_FINAL,
+            (pair_peers if pair else small_peers)[half][o],
+        )
+
+    def final_mine(mine, other):
         for o in OFFSETS:
+            final_copy(mine, o, False).start()
+
+    def final_other(mine, other):
+        for o in (2, 1, 3, 0):
+            final_copy(other, o, True).start()
+
+    all_finals = send(final_in, final_in, K_FINAL, partner)
+
+    def big_sum_send(t, half, offsets=OFFSETS):
+        for o in offsets:
             big_sum_copy(t, half, o).start()
 
     def decode_slot(t, after):
@@ -325,19 +367,17 @@
             for o in OFFSETS:
                 value = value + big_in[t, half, o - 1, i].astype(F32)
             r1[t, half, i] = value.astype(BF16)
+
+    def small_sum(half):
+        all_small_sums(half).wait_recv()
+        value = r1[1, half, small_pos[half]].astype(F32)
         for o in OFFSETS:
-            small_sum_copy(t, half, o).start()
-
-    def small_sum(t, half):
-        all_small_sums(t, half).wait_recv()
-        value = r1[t, half, small_pos[half]].astype(F32)
-        for o in OFFSETS:
-            value = value + small_in[t, half, o - 1].astype(F32)
-        r2[t, half] = value.astype(BF16)
+            value = value + small_in[half, o - 1].astype(F32)
+        r2[half] = value.astype(BF16)
 
     def cross_send(half, from_y):
         return send(
-            r2.at[1, half],
+            r2.at[half],
             cross_in.at[from_y],
             K_CROSS[from_y],
             place(x, 2 + half, z, core),
@@ -348,9 +388,11 @@
         decode_slot(1, lambda half: big_sum_send(1, half))
 
     def send_early(half):
+        big_sum_send(0, half, [o for o in OFFSETS if o not in HELD])
+
         @pl.when(second_layer)
         def _():
-            big_sum_send(0, half)
+            big_sum_send(0, half, HELD)
 
     decode_slot(0, send_early)
 
@@ -378,23 +420,31 @@
     def _():
         for half in HALVES:
             big_sum(1, half)
-        for half in HALVES:
-            big_sum_send(0, half)
-        for half in HALVES:
-            small_sum(1, half)
+            for o in OFFSETS:
+                small_sum_copy(half, o).start()
+        for half in HALVES:
+            big_sum_send(0, half, HELD)
+        for half in HALVES:
+            small_sum(half)
             for from_y in (0, 1):
 
                 @pl.when(yb == from_y)
                 def _():
                     cross_send(half, from_y).start()
 
-    for half in HALVES:
-        big_sum(0, half)
-
-    tok_y.wait_send()
-    tokens.drain()
+    def last_sums(mine, other):
+        big_sum(0, other)
+        final_other(mine, other)
+        big_sum(0, mine)
+        final_mine(mine, other)
+
+    by_half(last_sums)
+
+    tokens.drain(True)
     s0 = Gather(s, 0, K_GATHER[0])
-    s1 = Gather(s, 1, K_GATHER[1], (1, 3))
+    s1 = Gather(
+        s, 1, K_GATHER[1], [(1, 3) if half in PASS else OFFSETS for half in HALVES]
+    )
 
     def back_copy(to_y, half):
         big, small = block_at(half, z, x)
@@ -414,25 +464,11 @@
             place(x, 3 - y, z, core),
         )
 
-    @pl.when(first_layer)
-    def _():
-        for half in HALVES:
-            back_copy(0, half).wait_recv()
-            s1.small(half)
-
-    for half in HALVES:
-        small_sum(0, half)
-    y_copy = send(r2.at[0, 1 - yb], y_in, K_Y, y_pair)
-    y_copy.start()
-
-    @pl.when(first_layer)
-    def _():
-        for half in HALVES:
-            s1.big(half)
-
-    y_copy.wait_recv()
     tgt_copy.wait()
-    total = r2[0, yb].astype(F32) + y_in[...].astype(F32) - tgt[...].astype(F32)
+    all_finals.wait_recv()
+    total = r1[0, yb, block_at(yb, z, x)[1]].astype(F32) - tgt[...].astype(F32)
+    for i in range(7):
+        total = total + final_in[i].astype(F32)
     rerr[...] = total
 
     @pl.when(second_layer)
@@ -454,13 +490,7 @@
                 for to_y in (0, 1):
                     back_copy(to_y, half).start()
 
-    s_y = send(own_s, own_s, K_GATHER[0]["y"], y_pair)
-    s_y.start()
-
-    def s0_mine(mine, other):
-        s0.small(mine)
-
-    by_half(s0_mine)
+    by_half(s0.joint)
     rerr_copy = pltpu.make_async_copy(rerr, rerr_out, local_sem.at[11])
     rerr_copy.start()
 
@@ -471,14 +501,14 @@
             tile = tile + square[i * 8 : i * 8 + 8, j * 128 : j * 128 + 128]
 
     def square_copy(stage, o):
-        peers = (x_peers, z_peers, y_peers, [None, partner])[stage]
-        pos = (x, z, y, core)[stage]
+        peers = ([None, partner], y_peers, x_peers, z_peers)[stage]
+        pos = (core, y, x, z)[stage]
         return send(
             squares_own.at[stage], squares_in.at[stage, pos], K_SQUARE[stage], peers[o]
         )
 
     def square_offsets(stage):
-        return (1, 2, 3) if stage < 3 else (1,)
+        return (1, 2, 3) if stage > 0 else (1,)
 
     def all_squares(stage):
         ref = squares_in.at[stage, 0 : len(square_offsets(stage))]
@@ -486,27 +516,24 @@
 
     def squares_start(stage, value):
         squares_own[stage] = value
-        squares_in[stage, (x, z, y, core)[stage]] = value
+        squares_in[stage, (core, y, x, z)[stage]] = value
         for o in square_offsets(stage):
             square_copy(stage, o).start()
 
     def squares_end(stage):
         all_squares(stage).wait_recv()
         value = squares_in[stage, 0]
-        for i in range(1, 4 if stage < 3 else 2):
+        for i in range(1, 4 if stage > 0 else 2):
             value = value + squares_in[stage, i]
         return value
 
     squares_start(0, tile)
 
-    def feature_grad(t, from_core, n):
+    def feature_grad(t, n):
         rows = pl.ds(pl.multiple_of(n * 256, 256), 256)
-        weights = jnp.concatenate(
-            [decv[t, rows, cols] for cols in core_shards(from_core)], 1
-        )
         return rows, lax.dot_general(
-            core_columns(s, (t,), from_core),
-            weights,
+            all_columns(s, (t,)),
+            decv[t, rows, :],
             (((1,), (1,)), ((), ())),
             preferred_element_type=F32,
         )
@@ -515,43 +542,65 @@
         cols = pl.ds(pl.multiple_of(n * 256, 256), 256)
         return pltpu.make_async_copy(pg.at[:, cols], pg_out.at[:, cols], local_sem.at[7 + n])
 
-    def grad_start(t, from_core):
-        @pl.loop(0, 4)
+    def grad_first(t):
+        @pl.loop(0, 4, unroll=2)
         def _(n):
-            cols, value = feature_grad(t, from_core, n)
+            cols, value = feature_grad(t, n)
             fg[:, cols] = value
 
-    def grad_more(t, from_core):
-        @pl.loop(0, 4)
+    def grad_last(t, more):
+        @pl.loop(0, 4, unroll=2)
         def _(n):
-            cols, value = feature_grad(t, from_core, n)
-            fg[:, cols] = fg[:, cols] + value
-
-    def grad_end(t, from_core):
-        @pl.loop(0, 4)
-        def _(n):
-            cols, value = feature_grad(t, from_core, n)
-            grad = jnp.where(pre[:, cols] > 0.0, fg[:, cols] + value, 0.0).astype(BF16)
+            cols, value = feature_grad(t, n)
+            if more:
+                value = fg[:, cols] + value
+            grad = jnp.where(pre[:, cols] > 0.0, value, 0.0).astype(BF16)
             pg[:, cols] = grad
             bg[:, cols] = jnp.sum(grad.astype(F32), 0, keepdims=True)
             pg_copy(n).start()
 
-    def s0_other(mine, other):
-        s_y.wait_recv()
-        s0.small(other)
-
-    by_half(s0_other)
+    @pl.when(first_layer)
+    def _():
+        for half in HALVES:
+            back_copy(0, half).wait_recv()
+            s1.small(half)
+
     squares_start(1, squares_end(0))
-    by_half(big_hops(s0))
-
-    s_store0 = pltpu.make_async_copy(s.at[0], s_out.at[0], local_sem.at[5])
-    s_store1 = pltpu.make_async_copy(s.at[1], s_out.at[1], local_sem.at[6])
+    for t in ORDER:
+        if t == 0:
+            by_half(big_hops(s0))
+        else:
+
+            @pl.when(first_layer)
+            def _():
+                for half in HALVES:
+                    s1.big(half)
+
+    stores = [
+        pltpu.make_async_copy(s.at[t], s_out.at[t], local_sem.at[5 + t]) for t in (0, 1)
+    ]
+
+    def share_slot(t):
+        if t == 0:
+            for half in HALVES:
+                s0.share(half)
+        else:
+            for half in HALVES:
+                s1.share(half)
+            for half in PASS:
+                pass_copy(half).wait_recv()
+                s1.shared_copy(half, 2).start()
+
+    def done_slot(t):
+        (s0, s1)[t].done()
+        stores[t].start()
 
     @pl.when(second_layer)
     def _():
         for half in HALVES:
             s0.big_copy(half, 2).wait_recv()
-            pass_copy(half).start()
+            if half in PASS:
+                pass_copy(half).start()
             s0.shared_copy(half, 2).start()
         for half in HALVES:
             for o in (1, 3):
@@ -560,74 +609,66 @@
 
     @pl.when(first_layer)
     def _():
-        for half in HALVES:
-            s1.share(half)
+        share_slot(ORDER[0])
+        done_slot(ORDER[0])
 
     squares_start(2, squares_end(1))
-
-    @pl.when(first_layer)
-    def _():
-        for half in HALVES:
-            pass_copy(half).wait_recv()
-            s1.shared_copy(half, 2).start()
+    @pl.when(first_layer)
+    def _():
+        grad_first(ORDER[0])
+
+    @pl.when(first_layer)
+    def _():
+        share_slot(ORDER[1])
 
     squares_start(3, squares_end(2))
 
     @pl.when(first_layer)
     def _():
-        grad_start(1, core)
-
-    @pl.when(first_layer)
-    def _():
-        for half in HALVES:
-            s0.share(half)
-        s1.done()
-        s_store1.start()
-
-    @pl.when(first_layer)
-    def _():
-        grad_more(1, 1 - core)
-        grad_more(0, core)
+        done_slot(ORDER[1])
 
     @pl.when(second_layer)
     def _():
-        grad_start(0, core)
-
+        done_slot(0)
+
+    @pl.when(first_layer)
+    def _():
+        grad_last(ORDER[1], True)
+
+    @pl.when(second_layer)
+    def _():
+        grad_last(0, False)
+
+    bg_copy = pltpu.make_async_copy(bg, bg_out, local_sem.at[13])
+    bg_copy.start()
     squares_own[4] = squares_end(3)
     squares_copy = pltpu.make_async_copy(squares_own.at[4], squares_out, local_sem.at[12])
     squares_copy.start()
 
-    s0.done()
-    s_store0.start()
-    grad_end(0, 1 - core)
-    bg_copy = pltpu.make_async_copy(bg, bg_out, local_sem.at[13])
-    bg_copy.start()
-
     def drain_sums(t):
         for half in HALVES:
             part_copy(t, half).wait_send()
             all_big_sums(t, half).wait_send()
-            all_small_sums(t, half).wait_send()
 
     drain_sums(0)
-    y_copy.wait_send()
-    s_y.wait_send()
-    s0.drain()
+    all_finals.wait_send()
+    s0.drain(True)
     for stage in range(4):
         all_squares(stage).wait_send()
 
     @pl.when(first_layer)
     def _():
         drain_sums(1)
-        s1.drain()
-        for half in HALVES:
+        s1.drain(False)
+        for half in HALVES:
+            all_small_sums(half).wait_send()
             for from_y in (0, 1):
 
                 @pl.when(yb == from_y)
                 def _():
                     cross_send(half, from_y).wait_send()
 
-        s_store1.wait()
+        stores[1].wait()
 
     @pl.when(second_layer)
     def _():
@@ -638,9 +679,10 @@
                 for to_y in (0, 1):
                     back_copy(to_y, half).wait_send()
 
-            pass_copy(half).wait_send()
-
-    s_store0.wait()
+            if half in PASS:
+                pass_copy(half).wait_send()
+
+    stores[0].wait()
     rerr_copy.wait()
     squares_copy.wait()
     bg_copy.wait()
@@ -700,7 +742,7 @@
     def dec_half(t, half):
         s_copies[t][half].wait()
 
-        @pl.loop(0, 4, unroll=2)
+        @pl.loop(0, 4, unroll=4)
         def _(i):
             m = half * 4 + i
             block = column_block(s, (t,), half, lax.div(i, 2), lax.rem(i, 2))
@@ -739,7 +781,7 @@
             enc_out.at[rows, :], enc_grad.at[rows, :], enc_sem.at[n]
         )
 
-    @pl.loop(0, 4)
+    @pl.loop(0, 4, unroll=2)
     def _(n):
         rows = pl.ds(pl.multiple_of(n * 512, 512), 512)
         enc_out[rows, :] = jnp.dot(
@@ -787,9 +829,9 @@
             pltpu.VMEM((2, 2, 4, 4, ROWS, COLS), BF16),
             pltpu.VMEM((2, 2, 3, 4, ROWS, COLS), BF16),
             pltpu.VMEM((2, 2, 4, ROWS, COLS), BF16),
-            pltpu.VMEM((2, 2, 3, ROWS, COLS), BF16),
-            pltpu.VMEM((2, 2, ROWS, COLS), BF16),
-            pltpu.VMEM((ROWS, COLS), BF16),
+            pltpu.VMEM((2, 3, ROWS, COLS), BF16),
+            pltpu.VMEM((2, ROWS, COLS), BF16),
+            pltpu.VMEM((7, ROWS, COLS), BF16),
             pltpu.VMEM((2, ROWS, COLS), BF16),
             pltpu.VMEM((2, *blocks), BF16),
             pltpu.VMEM((TOK, SHARD), F32),

time: 88.9 us -> 80.4 us (0.904)
  Pallas kernels: 87.4 us -> 79.2 us
    pallas_call x1, Pallas kernels: 75.5 us -> 68.3 us  [on_device(): pl.pallas_call(step_kernel, out_shape=(shape((ROWS, COLS), F32), shape((8...]
    pallas_call x1, Pallas kernels: 11.9 us -> 10.9 us  [on_device(): pl.pallas_call(weight_grads_kernel, out_shape=(shape((2, SHARD, D), BF16)...]
where the time goes in v4:
time: 80.4 us; the launch traced here: 80 us
  Pallas kernels  79.2 us (99%)
    pallas_call x1, Pallas kernels, on_device(): pl.pallas_call(step_kernel, out_shape=(shape((ROWS, COLS), F32), shape((8...  68.3 us
    pallas_call x1, Pallas kernels, on_device(): pl.pallas_call(weight_grads_kernel, out_shape=(shape((2, SHARD, D), BF16)...  10.9 us

profile of v4, /device:TPU:1, one launch (start us, length us, event | category | flops | bytes accessed | tf_op | source)
XLA Modules:
  0.0 80.0 jit_solution(117279143365467614)
XLA Ops:
  0.6 68.3 %step.1 = (f32[64,256]{1,0:T(8,128)}, f32[8,128]{1,0:T(8,128)}, bf16[2048,512]{1,0:T(8,128)(2,1)}, bf16[1024,512]{1,0:T(8,128)(2,1)}, bf16[2,2,2,4,4,64,256]{6,5...) custom-call(bf16[64,256]{1,0:T(8,128)(2,1)} %tok.1, bf16[64,256]{1,0:T(8,128)(2,1)} %tgt_in.1, ...), custom_call_target="tpu_custom_call" | custom-call | tf_op jit(solution)/shard_map/step/pallas_call | solution.py:805
  69.0 10.9 %weight_grads.1 = (bf16[2,1024,2048]{2,1,0:T(8,128)(2,1)}, bf16[2048,1024]{1,0:T(8,128)(2,1)}, f32[64,256]{1,0:T(8,128)}, f32[1,1]{1,0:T(1,128)}, f32[1,1024]{1,0:T(1,128)}) custom-call(bf16[2048,512]{1,0:T(8,128)(2,1)} %get-tuple-element.17.gt_in, bf16[1024,512]{1,0:T(8,128)(2,1)} %get-tuple-element.18.ft_in, ...), custom_call_target="tpu_custom_call" | custom-call | tf_op jit(solution)/shard_map/weight_grads/pallas_call | solution.py:853

commit v5 on v4

--- a/solution.py
+++ b/solution.py
@@ -13,9 +13,12 @@
 COLS = 256
 LOSS_SCALE = 64.0
 MESH = pl.DeviceIdType.MESH
-HELD = (2,)
+FORWARD_TOKENS = False
+FORWARD_SCALED = False
 PASS = (0, 1)
 ORDER = (0, 1)
+EARLY = True
+EARLY1 = True
 BF16 = jnp.bfloat16
 F32 = jnp.float32
 
@@ -75,6 +78,7 @@
 
 K_GATHER = [gather_numbers(), gather_numbers()]
 K_PART = NUMBERS.take(2, 2)
+K_TURN = NUMBERS.take(2, 2)
 K_BIG = NUMBERS.take(2, 2)
 K_SMALL = NUMBERS.take(2)
 K_FINAL = NUMBERS.take()
@@ -88,7 +92,7 @@
 def step_kernel(
     tok, tgt_in, enc, bias_in, dec,
     rerr_out, squares_out, gt_out, ft_out, s_out, pg_out, bg_out,
-    tgt, bias, rerr, bg, encv, decv, g, pre, feat, p, rc, big_in, r1, small_in, r2, final_in, cross_in,
+    tgt, bias, rerr, bg, encv, decv, g, pre, feat, p, rc, turn_in, big_in, r1, small_in, r2, final_in, cross_in,
     s, fg, gt, ft, pg, squares_in, squares_own, send_sem, recv_sem, local_sem,
 ):
     me_layer = lax.axis_index("layer")
@@ -157,7 +161,10 @@
     pl.semaphore_wait(barrier, 16)
 
     class Gather:
-        def __init__(self, buf, t, numbers, offsets=(OFFSETS, OFFSETS)):
+        def __init__(self, buf, t, numbers, offsets=(OFFSETS, OFFSETS), forward=False):
+            self.forward = forward
+            if forward:
+                offsets = ((1, 3), (1, 3))
             self.buf, self.t, self.numbers = buf, t, numbers
             self.offsets = offsets
 
@@ -187,11 +194,21 @@
                 self.pair_copy(mine, o).start()
                 if o > 0:
                     self.small_copy(mine, o).start()
+            if EARLY:
+                self.early(mine)
 
         def big_copy(self, half, o):
             ref = self.chunk(half, big_pos[half])
             return send(ref, ref, self.numbers["big"][half][o], big_peers[half][o])
 
+        def piece_copy(self, half, o, i):
+            ref = self.buf.at[self.t, half, core, big_pos[half], i]
+            return send(ref, ref, self.numbers["big"][half][o], big_peers[half][o])
+
+        def early(self, half):
+            for o in self.offsets[half]:
+                self.piece_copy(half, o, small_pos[half]).start()
+
         def shared_copy(self, half, o):
             ref = self.chunk(half, turn(big_pos[half], 4 - o))
             return send(ref, ref, self.numbers["shared"], partner)
@@ -204,16 +221,31 @@
             for o in OFFSETS:
                 self.small_copy(half, o).start()
 
-        def big(self, half, count=3):
+        def big(self, half, count=3, early=False):
             self.all_small(half, count).wait_recv()
             for o in self.offsets[half]:
-                self.big_copy(half, o).start()
+                if not early:
+                    self.big_copy(half, o).start()
+                for d in OFFSETS if early else ():
+                    self.piece_copy(half, o, turn(small_pos[half], d)).start()
             self.shared_copy(half, 0).start()
+
+        def forward_copy(self, half, o):
+            part = pl.ds(0 if o == 1 else 2, 2)
+            ref = self.buf.at[self.t, half, core, turn(big_pos[half], 4 - o), part]
+            return send(ref, ref, self.numbers["big"][half][2], big_peers[half][o])
 
         def share(self, half):
             for o in self.offsets[half]:
                 self.big_copy(half, o).wait_recv()
+                if self.forward:
+                    self.forward_copy(half, o).start()
                 self.shared_copy(half, o).start()
+
+        def share_opposite(self, half):
+            if self.forward:
+                self.big_copy(half, 2).wait_recv()
+                self.shared_copy(half, 2).start()
 
         def done(self):
             self.all_shared(1 - core).wait_recv()
@@ -224,7 +256,7 @@
             for half in HALVES:
                 if not joint:
                     self.all_small(half).wait_send()
-                for o in self.offsets[half]:
+                for o in OFFSETS if self.forward else self.offsets[half]:
                     self.big_copy(half, o).wait_send()
             self.all_shared(core).wait_send()
 
@@ -237,12 +269,12 @@
         def _():
             fn(1, 0)
 
-    tokens = Gather(g, 0, K_GATHER[0])
+    tokens = Gather(g, 0, K_GATHER[0], forward=FORWARD_TOKENS)
     by_half(tokens.joint)
 
     def big_hops(gather):
         def run(mine, other):
-            gather.big(mine)
+            gather.big(mine, 3, EARLY)
             gather.big(other, 4)
 
         return run
@@ -253,6 +285,8 @@
         def run(mine, other):
             gather.share(mine)
             gather.share(other)
+            gather.share_opposite(mine)
+            gather.share_opposite(other)
 
         return run
 
@@ -307,16 +341,64 @@
                 p[t, half, core, b].astype(F32) + rc[t, half, b].astype(F32)
             ).astype(BF16)
 
-    def big_sum_copy(t, half, o):
-        return send(
-            p.at[t, half, core, turn(big_pos[half], o)],
-            big_in.at[t, half, o - 1],
-            K_BIG[t][half],
-            big_peers[half][o],
-        )
+    LOW, HIGH = pl.ds(0, 2), pl.ds(2, 2)
+
+    def chunk_sum(t, half, o, part):
+        return p.at[t, half, core, turn(big_pos[half], o), part]
+
+    def turn_copies(t, half):
+        return [
+            send(
+                chunk_sum(t, half, 2, part),
+                turn_in.at[t, half, i],
+                K_TURN[t][half],
+                big_peers[half][o],
+            )
+            for i, (part, o) in enumerate(((LOW, 1), (HIGH, 3)))
+        ]
+
+    def direct_copies(t, half):
+        return [
+            send(
+                chunk_sum(t, half, o, part), big_in.at[t, half, i], K_BIG[t][half], big_peers[half][o]
+            )
+            for i, part, o in ((0, LOW, 3), (2, HIGH, 1))
+        ]
+
+    def summed_copies(t, half):
+        return [
+            send(
+                chunk_sum(t, half, o, part), big_in.at[t, half, i], K_BIG[t][half], big_peers[half][o]
+            )
+            for i, part, o in ((1, LOW, 1), (3, HIGH, 3))
+        ]
+
+    def all_turns(t, half):
+        return send(turn_in.at[t, half], turn_in.at[t, half], K_TURN[t][half], partner)
 
     def all_big_sums(t, half):
-        return send(p.at[t, half, core, 0:3], big_in.at[t, half], K_BIG[t][half], partner)
+        return send(big_in.at[t, half], big_in.at[t, half], K_BIG[t][half], partner)
+
+    def big_start(t, half):
+        for copy in (*turn_copies(t, half), *direct_copies(t, half)):
+            copy.start()
+
+    def big_mid(t, half):
+        all_turns(t, half).wait_recv()
+        for i, (part, o) in enumerate(((LOW, 1), (HIGH, 3))):
+            ref = chunk_sum(t, half, o, part)
+            ref[...] = (ref[...].astype(F32) + turn_in[t, half, i].astype(F32)).astype(BF16)
+            summed_copies(t, half)[i].start()
+
+    def big_sum(t, half):
+        all_big_sums(t, half).wait_recv()
+        for i in range(4):
+            first = i // 2 * 2
+            r1[t, half, i] = (
+                p[t, half, core, big_pos[half], i].astype(F32)
+                + big_in[t, half, first, i % 2].astype(F32)
+                + big_in[t, half, first + 1, i % 2].astype(F32)
+            ).astype(BF16)
 
     def small_sum_copy(half, o):
         return send(
@@ -347,26 +429,19 @@
 
     all_finals = send(final_in, final_in, K_FINAL, partner)
 
-    def big_sum_send(t, half, offsets=OFFSETS):
-        for o in offsets:
-            big_sum_copy(t, half, o).start()
-
-    def decode_slot(t, after):
+    def decode_slot(t, between=None):
         for half in HALVES:
             decode(t, 1 - core, half)
             part_copy(t, half).start()
         for half in HALVES:
             decode(t, core, half)
             part_add(t, half)
-            after(half)
-
-    def big_sum(t, half):
-        all_big_sums(t, half).wait_recv()
-        for i in range(4):
-            value = p[t, half, core, big_pos[half], i].astype(F32)
-            for o in OFFSETS:
-                value = value + big_in[t, half, o - 1, i].astype(F32)
-            r1[t, half, i] = value.astype(BF16)
+            if between is None:
+                big_start(t, half)
+        if between is not None:
+            between()
+            for half in HALVES:
+                big_start(t, half)
 
     def small_sum(half):
         all_small_sums(half).wait_recv()
@@ -385,16 +460,15 @@
 
     @pl.when(first_layer)
     def _():
-        decode_slot(1, lambda half: big_sum_send(1, half))
-
-    def send_early(half):
-        big_sum_send(0, half, [o for o in OFFSETS if o not in HELD])
-
-        @pl.when(second_layer)
+        decode_slot(1)
+
+    def first_turns():
+        @pl.when(first_layer)
         def _():
-            big_sum_send(0, half, HELD)
-
-    decode_slot(0, send_early)
+            for half in HALVES:
+                big_mid(1, half)
+
+    decode_slot(0, first_turns)
 
     @pl.loop(0, 4)
     def _(n):
@@ -422,8 +496,12 @@
             big_sum(1, half)
             for o in OFFSETS:
                 small_sum_copy(half, o).start()
-        for half in HALVES:
-            big_sum_send(0, half, HELD)
+
+    for half in HALVES:
+        big_mid(0, half)
+
+    @pl.when(first_layer)
+    def _():
         for half in HALVES:
             small_sum(half)
             for from_y in (0, 1):
@@ -441,7 +519,7 @@
     by_half(last_sums)
 
     tokens.drain(True)
-    s0 = Gather(s, 0, K_GATHER[0])
+    s0 = Gather(s, 0, K_GATHER[0], forward=FORWARD_SCALED)
     s1 = Gather(
         s, 1, K_GATHER[1], [(1, 3) if half in PASS else OFFSETS for half in HALVES]
     )
@@ -538,6 +616,18 @@
             preferred_element_type=F32,
         )
 
+    def feature_grad_part(t, from_core, n):
+        rows = pl.ds(pl.multiple_of(n * 256, 256), 256)
+        weights = jnp.concatenate(
+            [decv[t, rows, cols] for cols in core_shards(from_core)], 1
+        )
+        return rows, lax.dot_general(
+            core_columns(s, (t,), from_core),
+            weights,
+            (((1,), (1,)), ((), ())),
+            preferred_element_type=F32,
+        )
+
     def pg_copy(n):
         cols = pl.ds(pl.multiple_of(n * 256, 256), 256)
         return pltpu.make_async_copy(pg.at[:, cols], pg_out.at[:, cols], local_sem.at[7 + n])
@@ -548,13 +638,17 @@
             cols, value = feature_grad(t, n)
             fg[:, cols] = value
 
-    def grad_last(t, more):
+    def grad_half(t, from_core, more):
         @pl.loop(0, 4, unroll=2)
         def _(n):
-            cols, value = feature_grad(t, n)
-            if more:
-                value = fg[:, cols] + value
-            grad = jnp.where(pre[:, cols] > 0.0, value, 0.0).astype(BF16)
+            cols, value = feature_grad_part(t, from_core, n)
+            fg[:, cols] = fg[:, cols] + value if more else value
+
+    def grad_last(t, from_core):
+        @pl.loop(0, 4, unroll=2)
+        def _(n):
+            cols, value = feature_grad_part(t, from_core, n)
+            grad = jnp.where(pre[:, cols] > 0.0, fg[:, cols] + value, 0.0).astype(BF16)
             pg[:, cols] = grad
             bg[:, cols] = jnp.sum(grad.astype(F32), 0, keepdims=True)
             pg_copy(n).start()
@@ -564,6 +658,8 @@
         for half in HALVES:
             back_copy(0, half).wait_recv()
             s1.small(half)
+            if EARLY1:
+                s1.early(half)
 
     squares_start(1, squares_end(0))
     for t in ORDER:
@@ -574,7 +670,7 @@
             @pl.when(first_layer)
             def _():
                 for half in HALVES:
-                    s1.big(half)
+                    s1.big(half, 3, EARLY1)
 
     stores = [
         pltpu.make_async_copy(s.at[t], s_out.at[t], local_sem.at[5 + t]) for t in (0, 1)
@@ -584,6 +680,8 @@
         if t == 0:
             for half in HALVES:
                 s0.share(half)
+            for half in HALVES:
+                s0.share_opposite(half)
         else:
             for half in HALVES:
                 s1.share(half)
@@ -597,15 +695,19 @@
 
     @pl.when(second_layer)
     def _():
+        if FORWARD_SCALED:
+            for half in HALVES:
+                s0.share(half)
         for half in HALVES:
             s0.big_copy(half, 2).wait_recv()
             if half in PASS:
                 pass_copy(half).start()
             s0.shared_copy(half, 2).start()
-        for half in HALVES:
-            for o in (1, 3):
-                s0.big_copy(half, o).wait_recv()
-                s0.shared_copy(half, o).start()
+        if not FORWARD_SCALED:
+            for half in HALVES:
+                for o in (1, 3):
+                    s0.big_copy(half, o).wait_recv()
+                    s0.shared_copy(half, o).start()
 
     @pl.when(first_layer)
     def _():
@@ -625,6 +727,15 @@
 
     @pl.when(first_layer)
     def _():
+        grad_half(ORDER[1], core, True)
+
+    @pl.when(second_layer)
+    def _():
+        grad_half(0, core, False)
+
+
+    @pl.when(first_layer)
+    def _():
         done_slot(ORDER[1])
 
     @pl.when(second_layer)
@@ -633,11 +744,11 @@
 
     @pl.when(first_layer)
     def _():
-        grad_last(ORDER[1], True)
+        grad_last(ORDER[1], 1 - core)
 
     @pl.when(second_layer)
     def _():
-        grad_last(0, False)
+        grad_last(0, 1 - core)
 
     bg_copy = pltpu.make_async_copy(bg, bg_out, local_sem.at[13])
     bg_copy.start()
@@ -648,6 +759,7 @@
     def drain_sums(t):
         for half in HALVES:
             part_copy(t, half).wait_send()
+            all_turns(t, half).wait_send()
             all_big_sums(t, half).wait_send()
 
     drain_sums(0)
@@ -715,13 +827,6 @@
     for copy in s_copies[0]:
         copy.start()
 
-    @pl.when(first_layer)
-    def _():
-        for copy in s_copies[1]:
-            copy.start()
-
-    pg_copy.start()
-    gt_copy.start()
     small_in = [
         pltpu.make_async_copy(src, dst, small_sem.at[i])
         for i, (src, dst) in enumerate(((rerr_in, rerr), (squares_in, squares), (bg_in, bg)))
@@ -730,8 +835,6 @@
         pltpu.make_async_copy(src, dst, small_sem.at[3 + i])
         for i, (src, dst) in enumerate(((rerr, rerr_out), (mean, mean_out), (bg, bg_out)))
     ]
-    for copy in small_in:
-        copy.start()
 
     def dec_copy(t, m):
         cols = pl.ds(pl.multiple_of(m * 256, 256), 256)
@@ -751,21 +854,31 @@
             ).astype(BF16)
             dec_copy(t, m).start()
 
+    ft_copy.wait()
+
+    @pl.when(first_layer)
+    def _():
+        for copy in s_copies[1]:
+            copy.start()
+
+    gt_copy.start()
+    pg_copy.start()
+    for copy in small_in:
+        copy.start()
+    dec_half(0, 0)
+    dec_half(0, 1)
+
+    @pl.when(first_layer)
+    def _():
+        dec_half(1, 0)
+        dec_half(1, 1)
+
     @pl.when(second_layer)
     def _():
         @pl.loop(0, 8)
         def _(m):
             dec_out[1, m] = jnp.zeros((SHARD, 256), BF16)
             dec_copy(1, m).start()
-
-    ft_copy.wait()
-    dec_half(0, 0)
-    dec_half(0, 1)
-
-    @pl.when(first_layer)
-    def _():
-        dec_half(1, 0)
-        dec_half(1, 1)
 
     for copy in small_in:
         copy.wait()
@@ -776,14 +889,14 @@
     gt_copy.wait()
 
     def enc_copy(n):
-        rows = pl.ds(pl.multiple_of(n * 512, 512), 512)
+        rows = pl.ds(pl.multiple_of(n * 256, 256), 256)
         return pltpu.make_async_copy(
             enc_out.at[rows, :], enc_grad.at[rows, :], enc_sem.at[n]
         )
 
-    @pl.loop(0, 4, unroll=2)
+    @pl.loop(0, 8, unroll=4)
     def _(n):
-        rows = pl.ds(pl.multiple_of(n * 512, 512), 512)
+        rows = pl.ds(pl.multiple_of(n * 256, 256), 256)
         enc_out[rows, :] = jnp.dot(
             gt[rows, :], pg[...], preferred_element_type=F32
         ).astype(BF16)
@@ -792,7 +905,7 @@
     for t in (0, 1):
         for m in range(8):
             dec_copy(t, m).wait()
-    for n in range(4):
+    for n in range(8):
         enc_copy(n).wait()
     for copy in small_out:
         copy.wait()
@@ -827,7 +940,8 @@
             pltpu.VMEM((TOK, SHARD), BF16),
             pltpu.VMEM((2, *blocks), BF16),
             pltpu.VMEM((2, 2, 4, 4, ROWS, COLS), BF16),
-            pltpu.VMEM((2, 2, 3, 4, ROWS, COLS), BF16),
+            pltpu.VMEM((2, 2, 2, 2, ROWS, COLS), BF16),
+            pltpu.VMEM((2, 2, 4, 2, ROWS, COLS), BF16),
             pltpu.VMEM((2, 2, 4, ROWS, COLS), BF16),
             pltpu.VMEM((2, 3, ROWS, COLS), BF16),
             pltpu.VMEM((2, ROWS, COLS), BF16),
@@ -874,7 +988,7 @@
             pltpu.VMEM((D, SHARD), BF16),
             pltpu.SemaphoreType.DMA((7,)),
             pltpu.SemaphoreType.DMA((2, 8)),
-            pltpu.SemaphoreType.DMA((4,)),
+            pltpu.SemaphoreType.DMA((8,)),
             pltpu.SemaphoreType.DMA((6,)),
         ],
         compiler_params=pltpu.CompilerParams(vmem_limit_bytes=60 * 2**20),

time: 80.4 us -> 78.3 us (0.974)
  Pallas kernels: 79.2 us -> 77.4 us
    pallas_call x1, Pallas kernels: 68.3 us -> 66.7 us  [on_device(): pl.pallas_call(step_kernel, out_shape=(shape((ROWS, COLS), F32), shape((8...]
where the time goes in v5:
time: 78.3 us; the launch traced here: 78.2 us
  Pallas kernels  77.4 us (99%)
  between operations  0.8 us (1%)
    pallas_call x1, Pallas kernels, on_device(): pl.pallas_call(step_kernel, out_shape=(shape((ROWS, COLS), F32), shape((8...  66.7 us
    pallas_call x1, Pallas kernels, on_device(): pl.pallas_call(weight_grads_kernel, out_shape=(shape((2, SHARD, D), BF16)...  10.7 us

profile of v5, /device:TPU:1, one launch (start us, length us, event | category | flops | bytes accessed | tf_op | source)
XLA Modules:
  0.0 78.2 jit_solution(7081836779101413897)
XLA Ops:
  0.6 66.7 %step.1 = (f32[64,256]{1,0:T(8,128)}, f32[8,128]{1,0:T(8,128)}, bf16[2048,512]{1,0:T(8,128)(2,1)}, bf16[1024,512]{1,0:T(8,128)(2,1)}, bf16[2,2,2,4,4,64,256]{6,5...) custom-call(bf16[64,256]{1,0:T(8,128)(2,1)} %tok.1, bf16[64,256]{1,0:T(8,128)(2,1)} %tgt_in.1, ...), custom_call_target="tpu_custom_call" | custom-call | tf_op jit(solution)/shard_map/step/pallas_call | solution.py:918
  67.3 10.7 %weight_grads.1 = (bf16[2,1024,2048]{2,1,0:T(8,128)(2,1)}, bf16[2048,1024]{1,0:T(8,128)(2,1)}, f32[64,256]{1,0:T(8,128)}, f32[1,1]{1,0:T(1,128)}, f32[1,1024]{1,0:T(1,128)}) custom-call(bf16[2048,512]{1,0:T(8,128)(2,1)} %get-tuple-element.17.gt_in, bf16[1024,512]{1,0:T(8,128)(2,1)} %get-tuple-element.18.ft_in, ...), custom_call_target="tpu_custom_call" | custom-call | tf_op jit(solution)/shard_map/weight_grads/pallas_call | solution.py:967

commit v6 on v5

--- a/solution.py
+++ b/solution.py
@@ -13,8 +13,6 @@
 COLS = 256
 LOSS_SCALE = 64.0
 MESH = pl.DeviceIdType.MESH
-FORWARD_TOKENS = False
-FORWARD_SCALED = False
 PASS = (0, 1)
 ORDER = (0, 1)
 EARLY = True
@@ -161,10 +159,7 @@
     pl.semaphore_wait(barrier, 16)
 
     class Gather:
-        def __init__(self, buf, t, numbers, offsets=(OFFSETS, OFFSETS), forward=False):
-            self.forward = forward
-            if forward:
-                offsets = ((1, 3), (1, 3))
+        def __init__(self, buf, t, numbers, offsets=(OFFSETS, OFFSETS)):
             self.buf, self.t, self.numbers = buf, t, numbers
             self.offsets = offsets
 
@@ -230,22 +225,10 @@
                     self.piece_copy(half, o, turn(small_pos[half], d)).start()
             self.shared_copy(half, 0).start()
 
-        def forward_copy(self, half, o):
-            part = pl.ds(0 if o == 1 else 2, 2)
-            ref = self.buf.at[self.t, half, core, turn(big_pos[half], 4 - o), part]
-            return send(ref, ref, self.numbers["big"][half][2], big_peers[half][o])
-
         def share(self, half):
             for o in self.offsets[half]:
                 self.big_copy(half, o).wait_recv()
-                if self.forward:
-                    self.forward_copy(half, o).start()
                 self.shared_copy(half, o).start()
-
-        def share_opposite(self, half):
-            if self.forward:
-                self.big_copy(half, 2).wait_recv()
-                self.shared_copy(half, 2).start()
 
         def done(self):
             self.all_shared(1 - core).wait_recv()
@@ -256,7 +239,7 @@
             for half in HALVES:
                 if not joint:
                     self.all_small(half).wait_send()
-                for o in OFFSETS if self.forward else self.offsets[half]:
+                for o in self.offsets[half]:
                     self.big_copy(half, o).wait_send()
             self.all_shared(core).wait_send()
 
@@ -269,7 +252,7 @@
         def _():
             fn(1, 0)
 
-    tokens = Gather(g, 0, K_GATHER[0], forward=FORWARD_TOKENS)
+    tokens = Gather(g, 0, K_GATHER[0])
     by_half(tokens.joint)
 
     def big_hops(gather):
@@ -285,8 +268,6 @@
         def run(mine, other):
             gather.share(mine)
             gather.share(other)
-            gather.share_opposite(mine)
-            gather.share_opposite(other)
 
         return run
 
@@ -301,14 +282,14 @@
             core_columns(g, (0,), from_core), weights, preferred_element_type=F32
         )
 
-    @pl.loop(0, 4, unroll=2)
+    @pl.loop(0, 4, unroll=4)
     def _(n):
         cols, value = encode_part(core, n)
         pre[:, cols] = value + bias[:, cols]
 
     tokens.done()
 
-    @pl.loop(0, 4, unroll=2)
+    @pl.loop(0, 4, unroll=4)
     def _(n):
         cols, value = encode_part(1 - core, n)
         act = pre[:, cols] + value
@@ -318,16 +299,19 @@
     dec_copy.wait()
 
     def decode(t, to_core, half):
+        firsts = [
+            pl.multiple_of((half * 4 + z_high * 2 + to_core) * 256, 256) for z_high in range(2)
+        ]
+        weights = jnp.concatenate([decv[t, :, pl.ds(first, 256)] for first in firsts], 1)
+        value = jnp.dot(feat[...], weights, preferred_element_type=F32).astype(BF16)
         for z_high in range(2):
-            first = pl.multiple_of((half * 4 + z_high * 2 + to_core) * 256, 256)
-            value = jnp.dot(
-                feat[...], decv[t, :, pl.ds(first, 256)], preferred_element_type=F32
-            ).astype(BF16)
             for to_x in range(4):
                 for z_low in range(2):
                     big, small = block_at(half, z_high * 2 + z_low, to_x)
                     at = (to_x * 2 + z_low) * ROWS
-                    p[t, half, to_core, big, small] = value[at : at + ROWS]
+                    p[t, half, to_core, big, small] = value[
+                        at : at + ROWS, z_high * 256 : z_high * 256 + 256
+                    ]
 
     def part_copy(t, half):
         return send(p.at[t, half, 1 - core], rc.at[t, half], K_PART[t][half], partner)
@@ -519,7 +503,7 @@
     by_half(last_sums)
 
     tokens.drain(True)
-    s0 = Gather(s, 0, K_GATHER[0], forward=FORWARD_SCALED)
+    s0 = Gather(s, 0, K_GATHER[0])
     s1 = Gather(
         s, 1, K_GATHER[1], [(1, 3) if half in PASS else OFFSETS for half in HALVES]
     )
@@ -633,19 +617,19 @@
         return pltpu.make_async_copy(pg.at[:, cols], pg_out.at[:, cols], local_sem.at[7 + n])
 
     def grad_first(t):
-        @pl.loop(0, 4, unroll=2)
+        @pl.loop(0, 4, unroll=4)
         def _(n):
             cols, value = feature_grad(t, n)
             fg[:, cols] = value
 
     def grad_half(t, from_core, more):
-        @pl.loop(0, 4, unroll=2)
+        @pl.loop(0, 4, unroll=4)
         def _(n):
             cols, value = feature_grad_part(t, from_core, n)
             fg[:, cols] = fg[:, cols] + value if more else value
 
     def grad_last(t, from_core):
-        @pl.loop(0, 4, unroll=2)
+        @pl.loop(0, 4, unroll=4)
         def _(n):
             cols, value = feature_grad_part(t, from_core, n)
             grad = jnp.where(pre[:, cols] > 0.0, fg[:, cols] + value, 0.0).astype(BF16)
@@ -680,8 +664,6 @@
         if t == 0:
             for half in HALVES:
                 s0.share(half)
-            for half in HALVES:
-                s0.share_opposite(half)
         else:
             for half in HALVES:
                 s1.share(half)
@@ -695,19 +677,15 @@
 
     @pl.when(second_layer)
     def _():
-        if FORWARD_SCALED:
-            for half in HALVES:
-                s0.share(half)
         for half in HALVES:
             s0.big_copy(half, 2).wait_recv()
             if half in PASS:
                 pass_copy(half).start()
             s0.shared_copy(half, 2).start()
-        if not FORWARD_SCALED:
-            for half in HALVES:
-                for o in (1, 3):
-                    s0.big_copy(half, o).wait_recv()
-                    s0.shared_copy(half, o).start()
+        for half in HALVES:
+            for o in (1, 3):
+                s0.big_copy(half, o).wait_recv()
+                s0.shared_copy(half, o).start()
 
     @pl.when(first_layer)
     def _():

time: 78.3 us -> 76.8 us (0.981)
  Pallas kernels: 77.4 us -> 75.9 us
    pallas_call x1, Pallas kernels: 66.7 us -> 65.1 us  [on_device(): pl.pallas_call(step_kernel, out_shape=(shape((ROWS, COLS), F32), shape((8...]
where the time goes in v6:
time: 76.8 us; the launch traced here: 76.7 us
  Pallas kernels  75.9 us (99%)
  between operations  0.8 us (1%)
    pallas_call x1, Pallas kernels, on_device(): pl.pallas_call(step_kernel, out_shape=(shape((ROWS, COLS), F32), shape((8...  65.1 us
    pallas_call x1, Pallas kernels, on_device(): pl.pallas_call(weight_grads_kernel, out_shape=(shape((2, SHARD, D), BF16)...  10.7 us

profile of v6, /device:TPU:1, one launch (start us, length us, event | category | flops | bytes accessed | tf_op | source)
XLA Modules:
  0.0 76.7 jit_solution(13072861960482225181)
XLA Ops:
  0.6 65.1 %step.1 = (f32[64,256]{1,0:T(8,128)}, f32[8,128]{1,0:T(8,128)}, bf16[2048,512]{1,0:T(8,128)(2,1)}, bf16[1024,512]{1,0:T(8,128)(2,1)}, bf16[2,2,2,4,4,64,256]{6,5...) custom-call(bf16[64,256]{1,0:T(8,128)(2,1)} %tok.1, bf16[64,256]{1,0:T(8,128)(2,1)} %tgt_in.1, ...), custom_call_target="tpu_custom_call" | custom-call | tf_op jit(solution)/shard_map/step/pallas_call | solution.py:896
  65.8 10.7 %weight_grads.1 = (bf16[2,1024,2048]{2,1,0:T(8,128)(2,1)}, bf16[2048,1024]{1,0:T(8,128)(2,1)}, f32[64,256]{1,0:T(8,128)}, f32[1,1]{1,0:T(1,128)}, f32[1,1024]{1,0:T(1,128)}) custom-call(bf16[2048,512]{1,0:T(8,128)(2,1)} %get-tuple-element.17.gt_in, bf16[1024,512]{1,0:T(8,128)(2,1)} %get-tuple-element.18.ft_in, ...), custom_call_target="tpu_custom_call" | custom-call | tf_op jit(solution)/shard_map/weight_grads/pallas_call | solution.py:945

commit v7 on v6

--- a/solution.py
+++ b/solution.py
@@ -16,7 +16,7 @@
 PASS = (0, 1)
 ORDER = (0, 1)
 EARLY = True
-EARLY1 = True
+EARLY1 = False
 BF16 = jnp.bfloat16
 F32 = jnp.float32
 
@@ -69,7 +69,7 @@
 def gather_numbers():
     return dict(
         small=NUMBERS.take(2),
-        big=NUMBERS.take(2, 4),
+        big=NUMBERS.take(2, 3),
         shared=NUMBERS.take(),
     )
 
@@ -124,7 +124,7 @@
         return pltpu.make_async_remote_copy(
             src_ref=src,
             dst_ref=dst,
-            send_sem=send_sem.at[number],
+            send_sem=send_sem,
             recv_sem=recv_sem.at[number],
             device_id=device,
             device_id_type=MESH,
@@ -194,11 +194,11 @@
 
         def big_copy(self, half, o):
             ref = self.chunk(half, big_pos[half])
-            return send(ref, ref, self.numbers["big"][half][o], big_peers[half][o])
+            return send(ref, ref, self.numbers["big"][half][o - 1], big_peers[half][o])
 
         def piece_copy(self, half, o, i):
             ref = self.buf.at[self.t, half, core, big_pos[half], i]
-            return send(ref, ref, self.numbers["big"][half][o], big_peers[half][o])
+            return send(ref, ref, self.numbers["big"][half][o - 1], big_peers[half][o])
 
         def early(self, half):
             for o in self.offsets[half]:
@@ -502,7 +502,6 @@
 
     by_half(last_sums)
 
-    tokens.drain(True)
     s0 = Gather(s, 0, K_GATHER[0])
     s1 = Gather(
         s, 1, K_GATHER[1], [(1, 3) if half in PASS else OFFSETS for half in HALVES]
@@ -740,6 +739,7 @@
             all_turns(t, half).wait_send()
             all_big_sums(t, half).wait_send()
 
+    tokens.drain(True)
     drain_sums(0)
     all_finals.wait_send()
     s0.drain(True)
@@ -786,12 +786,17 @@
     gt_in, ft_in, s_in, pg_in, rerr_in, squares_in, bg_in,
     dec_grad, enc_grad, rerr_out, mean_out, bg_out,
     gt, ft, s, pg, rerr, squares, mean, bg, dec_out, enc_out,
-    in_sem, dec_sem, enc_sem, small_sem,
+    first_sem, in_sem, dec_sem, enc_sem, small_sem,
 ):
     y = lax.div(lax.axis_index("layer"), 4)
     first_layer = y < 2
     second_layer = y >= 2
-    ft_copy = pltpu.make_async_copy(ft_in, ft, in_sem.at[0])
+    ft_copies = [
+        pltpu.make_async_copy(
+            ft_in.at[pl.ds(i * 256, 256)], ft.at[pl.ds(i * 256, 256)], first_sem.at[i]
+        )
+        for i in range(4)
+    ]
     s_copies = [
         [
             pltpu.make_async_copy(s_in.at[t, half], s.at[t, half], in_sem.at[1 + 2 * t + half])
@@ -801,8 +806,11 @@
     ]
     pg_copy = pltpu.make_async_copy(pg_in, pg, in_sem.at[5])
     gt_copy = pltpu.make_async_copy(gt_in, gt, in_sem.at[6])
-    ft_copy.start()
-    for copy in s_copies[0]:
+    first_s_copies = [
+        pltpu.make_async_copy(s_in.at[0, 0, c], s.at[0, 0, c], first_sem.at[4 + c])
+        for c in (0, 1)
+    ]
+    for copy in (*ft_copies, *first_s_copies, s_copies[0][1]):
         copy.start()
 
     small_in = [
@@ -821,7 +829,8 @@
         )
 
     def dec_half(t, half):
-        s_copies[t][half].wait()
+        if (t, half) != (0, 0):
+            s_copies[t][half].wait()
 
         @pl.loop(0, 4, unroll=4)
         def _(i):
@@ -832,7 +841,8 @@
             ).astype(BF16)
             dec_copy(t, m).start()
 
-    ft_copy.wait()
+    for copy in (*ft_copies, *first_s_copies):
+        copy.wait()
 
     @pl.when(first_layer)
     def _():
@@ -932,7 +942,7 @@
             pltpu.VMEM((TOK, SHARD), BF16),
             pltpu.VMEM((4, 4, 8, 128), F32),
             pltpu.VMEM((5, 8, 128), F32),
-            pltpu.SemaphoreType.DMA((K_COUNT,)),
+            pltpu.SemaphoreType.DMA,
             pltpu.SemaphoreType.DMA((K_COUNT,)),
             pltpu.SemaphoreType.DMA((14,)),
         ],
@@ -964,6 +974,7 @@
             pltpu.VMEM((1, SHARD), F32),
             pltpu.VMEM((2, 8, SHARD, 256), BF16),
             pltpu.VMEM((D, SHARD), BF16),
+            pltpu.SemaphoreType.DMA((6,)),
             pltpu.SemaphoreType.DMA((7,)),
             pltpu.SemaphoreType.DMA((2, 8)),
             pltpu.SemaphoreType.DMA((8,)),

time: 76.8 us -> 76.4 us (level)
  no operation moved by 1% of the time
where the time goes in v7:
time: 76.4 us; the launch traced here: 76.3 us
  Pallas kernels  75.5 us (99%)
  between operations  0.8 us (1%)
    pallas_call x1, Pallas kernels, on_device(): pl.pallas_call(step_kernel, out_shape=(shape((ROWS, COLS), F32), shape((8...  64.7 us
    pallas_call x1, Pallas kernels, on_device(): pl.pallas_call(weight_grads_kernel, out_shape=(shape((2, SHARD, D), BF16)...  10.8 us

profile of v7, /device:TPU:1, one launch (start us, length us, event | category | flops | bytes accessed | tf_op | source)
XLA Modules:
  0.0 76.3 jit_solution(5459685025471792120)
XLA Ops:
  0.6 64.7 %step.1 = (f32[64,256]{1,0:T(8,128)}, f32[8,128]{1,0:T(8,128)}, bf16[2048,512]{1,0:T(8,128)(2,1)}, bf16[1024,512]{1,0:T(8,128)(2,1)}, bf16[2,2,2,4,4,64,256]{6,5...) custom-call(bf16[64,256]{1,0:T(8,128)(2,1)} %tok.1, bf16[64,256]{1,0:T(8,128)(2,1)} %tgt_in.1, ...), custom_call_target="tpu_custom_call" | custom-call | tf_op jit(solution)/shard_map/step/pallas_call | solution.py:906
  65.3 10.8 %weight_grads.1 = (bf16[2,1024,2048]{2,1,0:T(8,128)(2,1)}, bf16[2048,1024]{1,0:T(8,128)(2,1)}, f32[64,256]{1,0:T(8,128)}, f32[1,1]{1,0:T(1,128)}, f32[1,1024]{1,0:T(1,128)}) custom-call(bf16[2048,512]{1,0:T(8,128)(2,1)} %get-tuple-element.17.gt_in, bf16[1024,512]{1,0:T(8,128)(2,1)} %get-tuple-element.18.ft_in, ...), custom_call_target="tpu_custom_call" | custom-call | tf_op jit(solution)/shard_map/weight_grads/pallas_call | solution.py:955
